TPU v7x, 32 devices: a whole 2x2x4 slice. The times are simulated.
32 devices in a mesh: dp: 8 (over z, x), seq: 4 (over y, core).
Axes of the slice: x: 2, y: 2, z: 4, core: 2. Of those that a mesh axis runs over, the one named last changes fastest.
Arguments:
- tokens: bfloat16 [2, 16384, 768], P(None, ('dp', 'seq')), may hold values from -6 to 6
- cotangent: bfloat16 [2, 16384, 768], P(None, ('dp', 'seq')), may hold values from -6 to 6
- lengths: int32 [2, 8, 4], P(None, 'dp'), may hold values from 1 to 1365, 2048 in all within a row
- gain_first: bfloat16 [768], P(('dp', 'seq')), may hold values from 0.5 to 1.5
- shift_first: bfloat16 [768], P(('dp', 'seq')), may hold values from -3 to 3
- packed_weight: bfloat16 [768, 2304], P(('dp', 'seq')), may hold values from -0.21875 to 0.21875
- packed_bias: bfloat16 [1536], P(('dp', 'seq')), may hold values from -3 to 3
- output_weight: bfloat16 [768, 768], P(('dp', 'seq')), may hold values from -6 to 6
- output_bias: bfloat16 [768], P(('dp', 'seq')), may hold values from -3 to 3
- gain_second: bfloat16 [768], P(('dp', 'seq')), may hold values from 0.5 to 1.5
- shift_second: bfloat16 [768], P(('dp', 'seq')), may hold values from -3 to 3
- expand_weight: bfloat16 [768, 3072], P(('dp', 'seq')), may hold values from -0.21875 to 0.21875
- expand_bias: bfloat16 [3072], P(('dp', 'seq')), may hold values from -3 to 3
- reduce_weight: bfloat16 [3072, 768], P(('dp', 'seq')), may hold values from -0.375 to 0.375
- reduce_bias: bfloat16 [768], P(('dp', 'seq')), may hold values from -3 to 3
Outputs:
- layer_output: bfloat16 [2, 16384, 768], P(None, ('dp', 'seq'))
- input_grad: bfloat16 [2, 16384, 768], P(None, ('dp', 'seq'))
- gain_first_grad: float32 [768], P(('dp', 'seq'))
- shift_first_grad: float32 [768], P(('dp', 'seq'))
- packed_weight_grad: float32 [768, 2304], P(('dp', 'seq'))
- packed_bias_grad: float32 [1536], P(('dp', 'seq'))
- output_weight_grad: float32 [768, 768], P(('dp', 'seq'))
- output_bias_grad: float32 [768], P(('dp', 'seq'))
- gain_second_grad: float32 [768], P(('dp', 'seq'))
- shift_second_grad: float32 [768], P(('dp', 'seq'))
- expand_weight_grad: float32 [768, 3072], P(('dp', 'seq'))
- expand_bias_grad: float32 [3072], P(('dp', 'seq'))
- reduce_weight_grad: float32 [3072, 768], P(('dp', 'seq'))
- reduce_bias_grad: float32 [768], P(('dp', 'seq'))
Inputs may be any that keep to these rules, and one draw needn't show every extreme that they name: Each row lengths[m, g] has 3 sequence lengths in order, then the padding length; it sums to 2048 and its largest entry is exactly 1365. Every entry, sequences and padding alike, lies anywhere from 1 to 1365; there is no larger lower bound. The padding mask is not an argument: it follows from the lengths.
All inputs are finite; a program needn't handle non-finite values.
Results may differ from a plain program's by a relative error of at most 0.011.
Values may be sent and summed in bfloat16 or wider, within the bound.
A program may use at most 192 MiB of HBM per device.

v0:
```python
import functools

import jax
import jax.numpy as jnp
from jax import lax
from jax.experimental import pallas as pl
from jax.experimental.pallas import tpu as pltpu
from jax.sharding import PartitionSpec as P

H = 12
HD = 64
BRANCH_SCALE = 12 ** (-0.5)
EPSILON = 1e-05
GELU_SCALE = 0.7978845608028654
GELU_CUBE = 0.044715
F32 = jnp.float32
BF16 = jnp.bfloat16
TILE = 256
PAIR = 2 * HD
MASKED = -1e30


def outer_sum(first, second):
    return lax.dot_general(first, second, (((0,), (0,)), ((), ())), preferred_element_type=F32)


def against_rows(first, second):
    return lax.dot_general(first, second, (((1,), (1,)), ((), ())), preferred_element_type=F32)


def layer_norm(values, norm_gain, norm_shift):
    center = values - jnp.mean(values, axis=-1, keepdims=True)
    spread = jnp.mean(center * center, axis=-1, keepdims=True)
    return center * lax.rsqrt(spread + EPSILON) * norm_gain + norm_shift


def gelu_and_slope(values):
    square = values * values
    bend = jnp.tanh(values * (GELU_SCALE + (GELU_SCALE * GELU_CUBE) * square))
    half = 0.5 + 0.5 * bend
    active = values * half
    slope = half + active * (1.0 - half) * (2.0 * GELU_SCALE + (6.0 * GELU_SCALE * GELU_CUBE) * square)
    return active, slope


def split_pair(rows):
    lane = lax.broadcasted_iota(jnp.int32, rows.shape, 1)
    nothing = jnp.zeros_like(rows)
    return jnp.where(lane < HD, rows, nothing), jnp.where(lane < HD, nothing, rows)


def third(packed, part, g):
    first = part * (packed.shape[1] // 3) + g * PAIR
    return slice(first, first + PAIR)


def allowed_in(key_block, row_block, begins, diagonal):
    keys = key_block * TILE + lax.broadcasted_iota(jnp.int32, (TILE, TILE), 0)
    allowed = keys >= begins
    if diagonal:
        rows = row_block * TILE + lax.broadcasted_iota(jnp.int32, (TILE, TILE), 1)
        allowed = allowed & (keys <= rows)
    return allowed


def attend_kernel(bounds_ref, packed_ref, begin_ref, out_ref, logsum_ref, value_t, held):
    blocks = packed_ref.shape[0] // TILE
    groups = out_ref.shape[1] // PAIR
    count = 2 * groups
    for g in range(groups):
        for block in range(blocks):
            at = slice(block * TILE, (block + 1) * TILE)
            value_t[g * PAIR : (g + 1) * PAIR, at] = packed_ref[at, third(packed_ref, 2, g)].T

    def one_row_block(i, carry):
        here = pl.ds(pl.multiple_of(i * TILE, TILE), TILE)
        begins = begin_ref[:, here]
        heads = []
        for g in range(groups):
            heads += split_pair(packed_ref[here, third(packed_ref, 0, g)] * HD ** (-0.5))

        def score(j, tops, masked, diagonal):
            there = pl.ds(pl.multiple_of(j * TILE, TILE), TILE)
            allowed = allowed_in(j, i, begins, diagonal) if masked else None
            new_tops = []
            for h in range(count):
                g = h // 2
                key_rows = packed_ref[there, third(packed_ref, 1, g)]
                scores = against_rows(key_rows, heads[h])
                if masked:
                    scores = jnp.where(allowed, scores, MASKED)
                held[h, there, :] = scores
                top = jnp.max(scores, axis=0, keepdims=True)
                new_tops.append(top if tops is None else jnp.maximum(top, tops[h]))
            return tuple(new_tops)

        tops = score(i, None, True, True)
        tops = lax.fori_loop(bounds_ref[0, i], bounds_ref[1, i], lambda j, s: score(j, s, True, False), tops)
        tops = lax.fori_loop(bounds_ref[1, i], i, lambda j, s: score(j, s, False, False), tops)

        def mix(j, state):
            there = pl.ds(pl.multiple_of(j * TILE, TILE), TILE)
            new_state = []
            for h in range(count):
                weights = jnp.exp(held[h, there, :] - tops[h])
                total, mixed = state[h]
                total = total + jnp.sum(weights, axis=0, keepdims=True)
                mixed = mixed + jnp.dot(
                    value_t[h * HD : (h + 1) * HD, there], weights.astype(BF16), preferred_element_type=F32
                )
                new_state.append((total, mixed))
            return tuple(new_state)

        empty = (jnp.zeros((1, TILE), F32), jnp.zeros((HD, TILE), F32))
        state = lax.fori_loop(bounds_ref[0, i], i + 1, mix, (empty,) * count)
        for g in range(groups):
            mixed = [mix / total for total, mix in state[2 * g : 2 * g + 2]]
            out_ref[here, g * PAIR : (g + 1) * PAIR] = jnp.concatenate(mixed, axis=0).T.astype(BF16)
        logs = [top + jnp.log(total) for top, (total, _) in zip(tops, state)]
        logsum_ref[:, here] = jnp.concatenate(logs, axis=0)
        return carry

    lax.fori_loop(0, blocks, one_row_block, 0)


def attend_forward(packed, low_blocks, begins):
    bucket, columns = packed.shape
    groups = columns // 3 // PAIR
    return pl.pallas_call(
        attend_kernel,
        name="attend_forward",
        out_shape=(
            jax.ShapeDtypeStruct((bucket, columns // 3), BF16),
            jax.ShapeDtypeStruct((2 * groups, bucket), F32),
        ),
        grid_spec=pltpu.PrefetchScalarGridSpec(
            num_scalar_prefetch=1,
            grid=(1,),
            in_specs=[
                pl.BlockSpec((bucket, columns), lambda g, low: (0, 0)),
                pl.BlockSpec((1, bucket), lambda g, low: (0, 0)),
            ],
            out_specs=[
                pl.BlockSpec((bucket, columns // 3), lambda g, low: (0, 0)),
                pl.BlockSpec((2 * groups, bucket), lambda g, low: (0, 0)),
            ],
            scratch_shapes=[
                pltpu.VMEM((groups * PAIR, bucket), BF16),
                pltpu.VMEM((2 * groups, bucket, TILE), F32),
            ],
        ),
        cost_estimate=pl.CostEstimate(
            flops=4 * 2 * groups * bucket * bucket * HD // 2,
            bytes_accessed=bucket * columns * 3,
            transcendentals=2 * groups * bucket * bucket // 2,
        ),
    )(low_blocks, packed, begins)


def attend_back_kernel(
    bounds_ref, packed_ref, o_ref, go_ref, begin_ref, logsum_ref, out_ref, key_t, query_t, delta
):
    blocks = packed_ref.shape[0] // TILE
    groups = o_ref.shape[1] // PAIR
    half = lax.broadcasted_iota(jnp.int32, (8, PAIR), 1) // HD
    picks = (half == lax.broadcasted_iota(jnp.int32, (8, PAIR), 0)).astype(F32).astype(BF16)
    for g in range(groups):
        column = slice(g * PAIR, (g + 1) * PAIR)
        for block in range(blocks):
            at = slice(block * TILE, (block + 1) * TILE)
            key_t[column, at] = packed_ref[at, third(packed_ref, 1, g)].T
            query_t[column, at] = jnp.zeros((PAIR, TILE), F32)
            product = o_ref[at, column].astype(F32) * go_ref[at, column].astype(F32)
            coarse = product.astype(BF16)
            fine = (product - coarse.astype(F32)).astype(BF16)
            delta[g * 8 : (g + 1) * 8, at] = against_rows(picks, coarse) + against_rows(picks, fine)

    def one_key_block(j, carry):
        there = pl.ds(pl.multiple_of(j * TILE, TILE), TILE)

        def visit(i, state, masked, diagonal):
            here = pl.ds(pl.multiple_of(i * TILE, TILE), TILE)
            allowed = allowed_in(j, i, begin_ref[:, here], diagonal) if masked else None
            new_state = []
            for g in range(groups):
                key_rows = packed_ref[there, third(packed_ref, 1, g)]
                value_rows = packed_ref[there, third(packed_ref, 2, g)]
                queries = split_pair(packed_ref[here, third(packed_ref, 0, g)] * HD ** (-0.5))
                grads = split_pair(go_ref[here, g * PAIR : (g + 1) * PAIR])
                key_grad, value_grad = state[g]
                for which in range(2):
                    h = 2 * g + which
                    scores = against_rows(key_rows, queries[which])
                    if masked:
                        scores = jnp.where(allowed, scores, MASKED)
                    probs = jnp.exp(scores - logsum_ref[h : h + 1, here])
                    grad_probs = against_rows(value_rows, grads[which])
                    row = 8 * g + which
                    grad_scores = (probs * (grad_probs - delta[row : row + 1, here])).astype(BF16)
                    value_grad = value_grad + jnp.dot(
                        probs.astype(BF16), grads[which], preferred_element_type=F32
                    )
                    key_grad = key_grad + jnp.dot(
                        grad_scores, queries[which], preferred_element_type=F32
                    )
                    at = slice(h * HD, (h + 1) * HD)
                    query_t[at, here] += jnp.dot(
                        key_t[at, there], grad_scores, preferred_element_type=F32
                    )
                new_state.append((key_grad, value_grad))
            return tuple(new_state)

        zero = jnp.zeros((TILE, PAIR), F32)
        state = visit(j, ((zero, zero),) * groups, True, True)
        state = lax.fori_loop(j + 1, bounds_ref[1, j], lambda i, s: visit(i, s, False, False), state)
        state = lax.fori_loop(bounds_ref[1, j], bounds_ref[0, j], lambda i, s: visit(i, s, True, False), state)
        for g in range(groups):
            out_ref[there, third(packed_ref, 1, g)] = state[g][0].astype(BF16)
            out_ref[there, third(packed_ref, 2, g)] = state[g][1].astype(BF16)
        return carry

    lax.fori_loop(0, blocks, one_key_block, 0)
    for g in range(groups):
        for block in range(blocks):
            at = slice(block * TILE, (block + 1) * TILE)
            rows = query_t[g * PAIR : (g + 1) * PAIR, at].T * HD ** (-0.5)
            out_ref[at, third(packed_ref, 0, g)] = rows.astype(BF16)


def attend_backward(packed, attended, grad_attended, logsum, high_blocks, begins):
    bucket, columns = packed.shape
    groups = columns // 3 // PAIR
    whole = lambda rows, width: pl.BlockSpec((rows, width), lambda g, high: (0, 0))
    return pl.pallas_call(
        attend_back_kernel,
        name="attend_backward",
        out_shape=jax.ShapeDtypeStruct((bucket, columns), BF16),
        grid_spec=pltpu.PrefetchScalarGridSpec(
            num_scalar_prefetch=1,
            grid=(1,),
            in_specs=[
                whole(bucket, columns),
                whole(bucket, columns // 3),
                whole(bucket, columns // 3),
                whole(1, bucket),
                whole(2 * groups, bucket),
            ],
            out_specs=whole(bucket, columns),
            scratch_shapes=[
                pltpu.VMEM((groups * PAIR, bucket), BF16),
                pltpu.VMEM((groups * PAIR, bucket), F32),
                pltpu.VMEM((groups * 8, bucket), F32),
            ],
        ),
        cost_estimate=pl.CostEstimate(
            flops=groups * bucket * bucket,
            bytes_accessed=bucket * columns,
            transcendentals=bucket,
        ),
    )(high_blocks, packed, attended, grad_attended, begins, logsum)


def position():
    dp, seq = lax.axis_index("dp"), lax.axis_index("seq")
    return lax.div(dp, 2), lax.rem(dp, 2), lax.div(seq, 2), lax.rem(seq, 2)


def device(z, x, y, core):
    return (2 * z + x, 2 * y + core)


def send(source, target, semaphores, index, to):
    leave, arrive = semaphores
    copy = pltpu.make_async_remote_copy(
        src_ref=source,
        dst_ref=target,
        send_sem=leave.at[index],
        recv_sem=arrive.at[index],
        device_id=to,
        device_id_type=pl.DeviceIdType.MESH,
    )
    copy.start()
    return copy


def meet(z, x, y, core):
    barrier = pltpu.get_barrier_semaphore()
    others = [device(z, 1 - x, y, core), device(z, x, 1 - y, core), device(z, x, y, 1 - core)]
    others += [device(lax.rem(z + t, 4), x, y, core) for t in (1, 2, 3)]
    for other in others:
        pl.semaphore_signal(barrier, inc=1, device_id=other, device_id_type=pl.DeviceIdType.MESH)
    pl.semaphore_wait(barrier, len(others))


def gather_kernel(
    token_ref, weight_ref, *rest
):
    vector_refs, (all_tokens, all_half, all_tiny, tiny_ref, local_sem), semaphores = rest[:8], rest[8:13], rest[13:]
    z, x, y, core = position()
    tiny_ref[...] = jnp.zeros_like(tiny_ref)
    for i, vector_ref in enumerate(vector_refs):
        tiny_ref[i, : vector_ref.shape[0]] = vector_ref[...].astype(F32)
    token_sems, half_sems, tiny_sems = [semaphores[2 * i : 2 * i + 2] for i in range(3)]
    meet(z, x, y, core)
    core_twin, y_twin, x_twin = device(z, x, y, 1 - core), device(z, x, 1 - y, core), device(z, 1 - x, y, core)
    columns = all_half.shape[5] // 3

    def weight_part(part, c):
        first = pl.multiple_of(part * 2 * columns + c * columns, PAIR)
        return weight_ref.at[:, pl.ds(first, columns)]

    streams = [(all_half, half_sems), (all_tiny, tiny_sems)]
    sent = []
    local = [
        pltpu.make_async_copy(token_ref.at[y], all_tokens.at[y, core], local_sem.at[0]),
        pltpu.make_async_copy(tiny_ref, all_tiny.at[z, x, y, core], local_sem.at[1]),
    ]
    swaps = [send(tiny_ref, all_tiny.at[z, x, y, core], tiny_sems, 0, core_twin)]
    for part in range(3):
        mine = all_half.at[z, x, y, core, :, part * columns : (part + 1) * columns]
        local.append(pltpu.make_async_copy(weight_part(part, core), mine, local_sem.at[2 + part]))
        swaps.append(send(weight_part(part, 1 - core), mine, half_sems, (0, 16, 17)[part], core_twin))
    for copy in local[1:] + local[:1]:
        copy.start()
    for copy in local[1:]:
        copy.wait()
    for copy in swaps:
        copy.wait_recv()
    sent += swaps
    own = [(whole.at[z, x, y], sems) for whole, sems in streams]
    over_y = [send(piece, piece, sems, 1, y_twin) for piece, sems in own]
    token_y = send(token_ref.at[1 - y], all_tokens.at[y, core], token_sems, 0, y_twin)
    token_own = send(token_ref.at[y], all_tokens.at[y, core], token_sems, 1, core_twin)
    along_z, over_x = {}, []

    def spread_piece(p, pieces):
        for t in (1, 2, 3):
            for i, (piece, sems) in enumerate(pieces):
                along_z[p, t, i] = send(piece, piece, sems, 1 + 3 * p + t, device(lax.rem(z + t, 4), x, y, core))
        for piece, sems in pieces:
            over_x.append(send(piece, piece, sems, 8 + 4 * p, x_twin))

    spread_piece(0, own)
    for copy in over_y:
        copy.wait_recv()
    spread_piece(1, [(whole.at[z, x, 1 - y], sems) for whole, sems in streams])
    token_y.wait_recv()
    token_next = send(all_tokens.at[1 - y, core], all_tokens.at[1 - y, core], token_sems, 2, core_twin)
    for p in (0, 1):
        row = y if p == 0 else 1 - y
        for t in (1, 2, 3):
            source = lax.rem(z + 4 - t, 4)
            for i, (whole, sems) in enumerate(streams):
                along_z[p, t, i].wait_recv()
                piece = whole.at[source, x, row]
                over_x.append(send(piece, piece, sems, 8 + 4 * p + t, x_twin))
    for copy in over_x + [token_own, token_next]:
        copy.wait_recv()
    for copy in sent + over_y + [token_y, token_own, token_next] + list(along_z.values()) + over_x:
        copy.wait_send()
    local[0].wait()


def gather_first(tokens, weight, vectors):
    _, local_rows, width = tokens.shape
    rows, columns = weight.shape
    anywhere = pl.BlockSpec(memory_space=pl.ANY)
    near = pl.BlockSpec(memory_space=pltpu.VMEM)
    sems = pltpu.SemaphoreType.DMA
    return pl.pallas_call(
        gather_kernel,
        name="gather_first",
        out_shape=(
            jax.ShapeDtypeStruct((2, 2, local_rows, width), BF16),
            jax.ShapeDtypeStruct((4, 2, 2, 2, rows, columns // 2), BF16),
            jax.ShapeDtypeStruct((4, 2, 2, 2, 8, 128), F32),
        ),
        in_specs=[near] * (2 + len(vectors)),
        out_specs=[anywhere] * 3,
        scratch_shapes=[pltpu.VMEM((8, 128), F32), sems((5,)), sems((3,)), sems((3,)), sems((18,)), sems((18,)), sems((16,)), sems((16,))],
        compiler_params=pltpu.CompilerParams(collective_id=1, has_side_effects=True),
    )(tokens, weight, *vectors)


def reduce_kernel(big_ref, flat_ref, tiny_ref, own_ref, other_ref, own_flat, other_flat, sum_ref, *scratch):
    z, x, y, core = position()
    meet(z, x, y, core)
    streams = []
    for i, source in enumerate((big_ref, flat_ref, tiny_ref)):
        streams.append((source,) + scratch[10 * i : 10 * i + 10])
    first_twin = device(z, x + (1 - core) * (1 - 2 * x), y + core * (1 - 2 * y), core)
    second_twin = device(z, x + core * (1 - 2 * x), y + (1 - core) * (1 - 2 * y), core)
    keep = (1 - core) * y + core * x
    order = (1, 2, 3, 0)
    one, two, three = {}, {}, {}
    for t in order:
        k = lax.rem(z + t, 4)
        for j in (0, 1):
            ix = (1 - core) * (1 - x) + core * j
            iy = (1 - core) * j + core * (1 - y)
            for i, (source, came_one, *_, leave, arrive) in enumerate(streams):
                one[t, j, i] = send(source.at[k, ix, iy], came_one.at[t, j], (leave, arrive), 2 * t + j, first_twin)
    for t in order:
        k = lax.rem(z + t, 4)
        for i, (source, came_one, sum_one, came_two, *_, leave, arrive) in enumerate(streams):
            for j in (0, 1):
                one[t, j, i].wait_recv()
                ix = (1 - core) * x + core * j
                iy = (1 - core) * j + core * y
                total = source[k, ix, iy].astype(F32) + came_one[t, j].astype(F32)
                sum_one[t, j] = total.astype(sum_one.dtype)
            two[t, i] = send(sum_one.at[t, 1 - keep], came_two.at[t], (leave, arrive), 8 + t, second_twin)
    for t in order:
        for i, (_, _, sum_one, came_two, sum_two, came_three, total_ref, _, leave, arrive) in enumerate(
            [(s[0], s[1], s[2], s[3], s[4], s[5], s[6], s[7], s[9], s[10]) for s in streams]
        ):
            two[t, i].wait_recv()
            total = sum_one[t, keep].astype(F32) + came_two[t].astype(F32)
            if t == 0:
                total_ref[...] = total
            else:
                sum_two[t - 1] = total.astype(sum_two.dtype)
                to = device(lax.rem(z + t, 4), x, y, core)
                three[t, i] = send(sum_two.at[t - 1], came_three.at[t - 1], (leave, arrive), 11 + t, to)
    last = []
    for i, s in enumerate(streams):
        came_three, total_ref, came_last, leave, arrive = s[5], s[6], s[7], s[9], s[10]
        for t in (1, 2, 3):
            three[t, i].wait_recv()
        total_ref[...] += sum(came_three[t].astype(F32) for t in range(3))
        rows = came_last.shape[0]
        piece = total_ref.at[pl.ds(pl.multiple_of((1 - core) * rows, 8), rows)]
        last.append(send(piece, came_last, (leave, arrive), 15, device(z, x, y, 1 - core)))
    rows = own_ref.shape[0]
    mine = pl.ds(pl.multiple_of(core * rows, 8), rows)
    own_ref[...] = streams[0][6][mine]
    own_flat[...] = streams[1][6][mine]
    for copy in last:
        copy.wait_recv()
    other_ref[...] = streams[0][7][...]
    other_flat[...] = streams[1][7][...]
    sum_ref[...] = streams[2][6][pl.ds(pl.multiple_of(core * 8, 8), 8)] + streams[2][7][...]
    for copy in list(one.values()) + list(two.values()) + list(three.values()) + last:
        copy.wait_send()


def reduce_last(big, flat, tiny):
    rows, half_columns = big.shape[3:]
    flat_columns = flat.shape[4]
    near = pl.BlockSpec(memory_space=pltpu.VMEM)
    scratch = []
    for shape, kind, kept in (
        ((rows, half_columns), BF16, (rows // 2, half_columns)),
        ((rows, flat_columns), BF16, (rows // 2, flat_columns)),
        ((16, 128), F32, (8, 128)),
    ):
        scratch += [
            pltpu.VMEM((4, 2) + shape, kind),
            pltpu.VMEM((4, 2) + shape, kind),
            pltpu.VMEM((4,) + shape, kind),
            pltpu.VMEM((3,) + shape, kind),
            pltpu.VMEM((3,) + shape, kind),
            pltpu.VMEM(shape, F32),
            pltpu.VMEM(kept, F32),
            pltpu.SemaphoreType.DMA((1,)),
            pltpu.SemaphoreType.DMA((16,)),
            pltpu.SemaphoreType.DMA((16,)),
        ]
    return pl.pallas_call(
        reduce_kernel,
        name="reduce_last",
        out_shape=(
            jax.ShapeDtypeStruct((rows // 2, half_columns), F32),
            jax.ShapeDtypeStruct((rows // 2, half_columns), F32),
            jax.ShapeDtypeStruct((rows // 2, flat_columns), F32),
            jax.ShapeDtypeStruct((rows // 2, flat_columns), F32),
            jax.ShapeDtypeStruct((8, 128), F32),
        ),
        in_specs=[near] * 3,
        out_specs=[near] * 5,
        scratch_shapes=scratch,
        compiler_params=pltpu.CompilerParams(collective_id=2, has_side_effects=True),
    )(big, flat, tiny)


def pack_kernel(output_ref, expand_ref, reduce_ref, out_ref):
    width = output_ref.shape[1]
    count = expand_ref.shape[1] // width
    out_ref[0] = output_ref[...]
    for j in range(count):
        out_ref[1 + j] = expand_ref[:, j * width : (j + 1) * width]
        out_ref[1 + count + j] = reduce_ref[j]


def pack_second(output_weight, expand_weight, reduce_weight):
    rows, width = output_weight.shape
    count = expand_weight.shape[1] // width
    near = pl.BlockSpec(memory_space=pltpu.VMEM)
    packed = pl.pallas_call(
        pack_kernel,
        name="pack_second",
        out_shape=jax.ShapeDtypeStruct((1 + 2 * count, rows, width), BF16),
        in_specs=[near] * 3,
        out_specs=near,
    )(output_weight, expand_weight, reduce_weight.reshape(count, rows, width))
    return packed.reshape(-1, width)


def gather_rows(shard):
    return lax.all_gather(shard, ("dp", "seq"), axis=0, tiled=True)


def scatter_sum(full):
    return lax.psum_scatter(full, ("dp", "seq"), scatter_dimension=0, tiled=True)


def local(
    tokens,
    cotangent,
    lengths,
    gain_first,
    shift_first,
    packed_weight,
    packed_bias,
    output_weight,
    output_bias,
    gain_second,
    shift_second,
    expand_weight,
    expand_bias,
    reduce_weight,
    reduce_bias,
):
    micro_count, local_rows, width = tokens.shape
    groups = lax.axis_size("seq")
    devices = groups * lax.axis_size("dp")
    share = groups // micro_count
    bucket = local_rows * groups
    hidden_width = expand_weight.shape[1]
    columns = width // share
    place = lax.axis_index("seq")
    mine, core = place // share, place % share
    swap_micro = [(s, (s + share) % groups) for s in range(groups)]
    swap_core = [(s, s ^ 1) for s in range(groups)]

    def swap_of(both):
        return lax.dynamic_index_in_dim(both, 1 - mine, 0, keepdims=False)

    def placed(both, came):
        kept = lax.dynamic_index_in_dim(both, mine, 0, keepdims=False)
        return jnp.stack([jnp.where(mine == 0, kept, came), jnp.where(mine == 0, came, kept)])

    def own_micro(both):
        return placed(both, lax.ppermute(swap_of(both), "seq", swap_micro))

    def home_micro(blocks):
        kept = lax.dynamic_index_in_dim(blocks, mine, 0, keepdims=False)
        sent = lax.dynamic_index_in_dim(blocks, 1 - mine, 0, keepdims=False)
        came = lax.ppermute(sent, "seq", swap_micro)
        return jnp.stack([jnp.where(mine == 0, kept, came), jnp.where(mine == 0, came, kept)])

    def interleave(own, other):
        first, second = jnp.where(core == 0, own, other), jnp.where(core == 0, other, own)
        return jnp.stack([first, second], axis=1).reshape((bucket,) + own.shape[2:])


    vectors = (gain_first, shift_first, packed_bias, output_bias, gain_second, shift_second, expand_bias, reduce_bias)
    sizes = [v.shape[0] for v in vectors]
    small_count = sum(sizes)
    pieces_per_row = hidden_width // width
    rows = output_weight.shape[0]
    own_kernels = devices == 32 and groups == 4
    if own_kernels:
        all_tokens, half_packed, all_tiny = gather_first(tokens, packed_weight, vectors)
        everyone = all_tokens.reshape(bucket, width)
        own_tokens = lax.dynamic_index_in_dim(all_tokens, core, 1, keepdims=False)
        half_packed = half_packed.reshape(width, 3 * columns)
    else:
        own_tokens = own_micro(tokens)
        everyone = interleave(own_tokens, lax.ppermute(own_tokens, "seq", swap_core))
        full_packed = gather_rows(packed_weight)
        half_packed = jnp.concatenate(
            [lax.dynamic_slice(full_packed, (0, part * width + core * columns), (width, columns)) for part in range(3)], axis=1
        )
        tiny = jnp.concatenate([jnp.pad(v.astype(F32), (0, 128 - v.shape[0])) for v in vectors]).reshape(8, 128)
        all_tiny = gather_rows(tiny)
    small_all = all_tiny.reshape(devices, 8, 128)
    if own_kernels:
        second_shard = pack_second(output_weight, expand_weight, reduce_weight)
    else:
        expand_blocks = [expand_weight[:, j * width : (j + 1) * width] for j in range(pieces_per_row)]
        second_shard = jnp.concatenate([output_weight] + expand_blocks + [reduce_weight])
    second = gather_rows(second_shard).reshape(devices, -1, width)
    full_output = second[:, :rows].reshape(width, width)
    full_expand = jnp.concatenate(
        [second[:, rows * (j + 1) : rows * (j + 2)].reshape(width, width) for j in range(pieces_per_row)], axis=1
    )
    full_reduce = second[:, rows * (pieces_per_row + 1) :].reshape(hidden_width, width)
    pieces = [small_all[:, i, :size].reshape(-1) for i, size in enumerate(sizes)]
    gain_one, shift_one, packed_shift, output_shift, gain_two, shift_two, expand_shift, reduce_shift = pieces

    places = jnp.arange(bucket, dtype=jnp.int32)
    bucket_lengths = lax.dynamic_index_in_dim(lengths, mine, 0, keepdims=False)[0]
    slot_count = lengths.shape[-1]
    ends = jnp.cumsum(bucket_lengths)
    past = (places[:, None] >= ends[None, :]).astype(jnp.int32)
    begins = jnp.sum(past * bucket_lengths[None, :], axis=1)
    block_ids = jnp.arange(bucket // TILE, dtype=jnp.int32)
    first_begin, last_begin = begins[::TILE], begins[TILE - 1 :: TILE]
    low = first_begin // TILE
    low_blocks = jnp.stack([low, jnp.minimum(-(-last_begin // TILE), block_ids)])
    high = jnp.sum((low[None, :] <= block_ids[:, None]).astype(jnp.int32), axis=1)
    free = jnp.sum((last_begin[None, :] <= block_ids[:, None] * TILE).astype(jnp.int32), axis=1)
    high_blocks = jnp.stack([high, jnp.clip(free, block_ids + 1, high)])
    begins = begins[None, :]
    valid_all = (jnp.sum(past, axis=1) < slot_count - 1).astype(F32).reshape(2, share, local_rows)
    valid = lax.dynamic_index_in_dim(valid_all, core, 1, keepdims=False).reshape(-1, 1)

    inputs = own_tokens.reshape(-1, width).astype(F32)
    normed_low = layer_norm(everyone.astype(F32), gain_one, shift_one).astype(BF16)
    bias_row = jnp.concatenate([packed_shift[:width], jnp.zeros((width,), F32), packed_shift[width:]])
    half_bias = jnp.concatenate(
        [lax.dynamic_slice(bias_row, (part * width + core * columns,), (columns,)) for part in range(3)]
    )
    packed = (jnp.dot(normed_low, half_packed, preferred_element_type=F32) + half_bias).astype(BF16)
    packed, cotangent_sent = lax.optimization_barrier((packed, swap_of(cotangent)))
    attended_heads, logsum = attend_forward(packed, low_blocks, begins)
    attended_heads, cotangent_came = lax.optimization_barrier(
        (attended_heads, lax.ppermute(cotangent_sent, "seq", swap_micro))
    )
    own_cotangent = placed(cotangent, cotangent_came)

    by_core = attended_heads.reshape(2, share, local_rows, columns)
    kept = lax.dynamic_index_in_dim(by_core, core, 1, keepdims=False)
    came = lax.ppermute(lax.dynamic_index_in_dim(by_core, 1 - core, 1, keepdims=False), "seq", swap_core)
    attended = jnp.concatenate(
        [jnp.where(core == 0, kept, came), jnp.where(core == 0, came, kept)], axis=-1
    ).reshape(-1, width)

    middle = inputs + BRANCH_SCALE * (
        jnp.dot(attended, full_output, preferred_element_type=F32) + output_shift
    )
    normed_two, norm_back_two = jax.vjp(layer_norm, middle, gain_two, shift_two)
    normed_two_low = normed_two.astype(BF16)
    activated, slope = gelu_and_slope(
        jnp.dot(normed_two_low, full_expand, preferred_element_type=F32) + expand_shift
    )
    active_low, slope_low = lax.optimization_barrier((activated.astype(BF16), slope.astype(BF16)))
    branch_out = jnp.dot(active_low, full_reduce, preferred_element_type=F32) + reduce_shift
    layer_rows = ((middle + BRANCH_SCALE * branch_out) * valid).astype(BF16)

    grad_rows = own_cotangent.reshape(-1, width).astype(F32) * valid
    grad_branch = (BRANCH_SCALE * grad_rows).astype(BF16)
    reduce_weight_grad = outer_sum(active_low, grad_branch)
    reduce_bias_grad = jnp.sum(grad_branch.astype(F32), axis=0)
    grad_hidden = (against_rows(grad_branch, full_reduce) * slope_low.astype(F32)).astype(BF16)
    expand_weight_grad = outer_sum(normed_two_low, grad_hidden)
    expand_bias_grad = jnp.sum(grad_hidden.astype(F32), axis=0)
    early = jnp.concatenate(
        [
            expand_weight_grad[:, j * width : (j + 1) * width].astype(BF16).reshape(devices, rows, width)
            for j in range(pieces_per_row)
        ]
        + [reduce_weight_grad.astype(BF16).reshape(devices, -1, width)],
        axis=1,
    )
    early, grad_hidden = lax.optimization_barrier((early, grad_hidden))
    early_sum = scatter_sum(early.reshape(-1, width)).astype(F32)
    middle_part, gain_two_grad, shift_two_grad = norm_back_two(against_rows(grad_hidden, full_expand))
    grad_middle = grad_rows + middle_part
    grad_proj = (BRANCH_SCALE * grad_middle).astype(BF16)
    output_weight_grad = outer_sum(attended, grad_proj).astype(BF16)
    output_bias_grad = jnp.sum(grad_proj.astype(F32), axis=0)
    grad_attended = against_rows(grad_proj, full_output).astype(BF16)
    take = lambda c: lax.dynamic_slice(grad_attended, (0, c * columns), (2 * local_rows, columns))
    kept = take(core).reshape(2, local_rows, columns)
    came = lax.ppermute(take(1 - core), "seq", swap_core).reshape(2, local_rows, columns)
    grad_heads = interleave(kept, came)
    grad_packed = attend_backward(packed, attended_heads, grad_heads, logsum, high_blocks, begins)
    half_grad = outer_sum(normed_low, grad_packed).astype(BF16)
    half_sums = jnp.sum(grad_packed.astype(F32), axis=0).reshape(3, columns)
    part_grad = against_rows(grad_packed, half_packed).astype(BF16)
    by_core = part_grad.reshape(2, share, local_rows, width)
    kept = lax.dynamic_index_in_dim(by_core, core, 1, keepdims=False)
    came = lax.ppermute(lax.dynamic_index_in_dim(by_core, 1 - core, 1, keepdims=False), "seq", swap_core)
    norm_grad = (kept.astype(F32) + came.astype(F32)).reshape(-1, width)
    _, norm_back_one = jax.vjp(layer_norm, inputs, gain_one, shift_one)
    input_part, gain_one_grad, shift_one_grad = norm_back_one(norm_grad)
    input_rows = (grad_middle + input_part).astype(BF16)

    layer_output = home_micro(layer_rows.reshape(2, local_rows, width))
    input_grad = home_micro(input_rows.reshape(2, local_rows, width))

    def spread(half):
        nothing = jnp.zeros_like(half)
        return [jnp.where(core == place_of, half, nothing) for place_of in range(share)]

    packed_bias_grad = jnp.concatenate([block for part in (0, 2) for block in spread(half_sums[part])])
    small_grads = [gain_one_grad, shift_one_grad, packed_bias_grad, output_bias_grad, gain_two_grad, shift_two_grad, expand_bias_grad, reduce_bias_grad]
    if own_kernels:
        small_rows = jnp.stack(
            [jnp.pad(g.reshape(devices, -1), ((0, 0), (0, 128 - g.size // devices))) for g in small_grads], axis=1
        ).reshape(4, 2, 2, share * 8, 128)
        half_output = lambda c: lax.dynamic_slice(output_weight_grad, (0, c * columns), (width, columns))
        came = lax.ppermute(half_output(1 - core), "seq", swap_core)
        flat = (half_output(core).astype(F32) + came.astype(F32)).astype(BF16)
        own_half, other_half, own_flat, other_flat, small_sum = reduce_last(
            half_grad.reshape(4, 2, 2, share * rows, 3 * columns), flat.reshape(4, 2, 2, share * rows, columns), small_rows
        )
        output_sum = jnp.concatenate([jnp.where(core == c, own_flat, other_flat) for c in range(share)], axis=1)
        packed_halves = [jnp.where(core == c, own_half, other_half) for c in range(share)]
        pieces = [small_sum[i, :size] for i, size in enumerate(sizes)]
    else:
        output_sum = scatter_sum(output_weight_grad).astype(F32)
        both_halves = scatter_sum(jnp.concatenate(spread(half_grad), axis=1)).astype(F32)
        packed_halves = [both_halves[:, c * 3 * columns : (c + 1) * 3 * columns] for c in range(share)]
        small_sum = scatter_sum(jnp.concatenate([g.reshape(devices, -1) for g in small_grads], axis=1))[0]
        pieces, at = [], 0
        for size in sizes:
            pieces.append(small_sum[at : at + size])
            at += size
    packed_sum = jnp.concatenate(
        [
            packed_halves[c][:, part * columns : (part + 1) * columns]
            for part in range(3)
            for c in range(share)
        ],
        axis=1,
    )
    expand_sum = jnp.concatenate(
        [early_sum[rows * j : rows * (j + 1)] for j in range(pieces_per_row)], axis=1
    )
    big = (early_sum[rows * pieces_per_row :], expand_sum, output_sum, packed_sum)
    return (
        layer_output,
        input_grad,
        pieces[0],
        pieces[1],
        big[3],
        pieces[2],
        big[2],
        pieces[3],
        pieces[4],
        pieces[5],
        big[1],
        pieces[6],
        big[0],
        pieces[7],
    )


def solution(mesh):
    both = ("dp", "seq")
    token_spec = P(None, both, None)
    vector, matrix = P(both), P(both, None)
    in_specs = (
        token_spec,
        token_spec,
        P(None, "dp", None),
        vector,
        vector,
        matrix,
        vector,
        matrix,
        vector,
        vector,
        vector,
        matrix,
        vector,
        matrix,
        vector,
    )
    out_specs = (
        token_spec,
        token_spec,
        vector,
        vector,
        matrix,
        vector,
        matrix,
        vector,
        vector,
        vector,
        matrix,
        vector,
        matrix,
        vector,
    )
    return jax.shard_map(local, mesh=mesh, in_specs=in_specs, out_specs=out_specs, check_vma=False)
```

profile of v0, /device:TPU:9, one launch (start us, length us, event | category | flops | bytes accessed | tf_op | source)
XLA Modules:
  0.0 378.6 jit_solution(10111711835467776976)
XLA Ops:
  7.2 1.8 pack_second.1
  9.1 55.4 %gather_first.1 = (bf16[2,2,512,768]{3,2,1,0:T(8,128)(2,1)}, bf16[4,2,2,2,24,1152]{5,4,3,2,1,0:T(8,128)(2,1)}, f32[4,2,2,2,8,128]{5,4,3,2,1,0:T(8,128)}) custom-call(bf16[2,512,768]{2,1,0:T(8,128)(2,1)} %token_ref.1, bf16[24,2304]{1,0:T(8,128)(2,1)} %weight_ref.1, bf16[24]{0:T(256)(128)(2,1)} %rest_0_.1, bf16[24]{0:T(256)(128)(2,1)} %rest_1_.1, ...), custom_call_target="tpu_custom_call" | custom-call | tf_op jit(solution)/shard_map/gather_first/pallas_call | solution.py:370
  64.5 1.4 fusion.43
  67.3 2.1 dynamic-slice_bitcast_fusion.4
  69.4 2.4 convert_reduce_fusion.2
  72.9 1.5 add_convert_fusion.2
  74.4 5.8 %add_convert_fusion.1.packed_ref = bf16[2048,1152]{1,0:T(8,128)(2,1)} fusion(bf16[2048,768]{1,0:T(8,128)(2,1)S(1)} %bitcast.270, bf16[768,1152]{1,0:T(8,128)(2,1)S(1)} %bitcast.321, f32[1152]{0:T(1024)S(1)} %pad_maximum_fusion.11), kind=kOutput, calls=%fused_computation.7 | convolution fusion | flops 3628597248 | bytes 9638400 | tf_op jit(solution)/shard_map/dot_general | solution.py:625
  83.0 26.4 %attend_forward.1 = (bf16[2048,384]{1,0:T(8,128)(2,1)}, f32[6,2048]{1,0:T(8,128)}) custom-call(s32[2,8]{1,0:T(2,128)} %get-tuple-element.135.bounds_ref, bf16[2048,1152]{1,0:T(8,128)(2,1)} %add_convert_fusion.1.packed_ref, s32[1,2048]{1,0:T(1,128)} %bitcast.311), custom_call_target="tpu_custom_call" | custom-call | flops 3221225472 | bytes 7077888 | tf_op jit(solution)/shard_map/attend_forward/pallas_call | solution.py:129
  109.9 1.3 constant_dynamic-slice_fusion.4
  111.2 2.5 fusion.5
  113.7 1.6 collective-permute-done
  117.3 1.2 fusion.23
  119.5 1.7 convert_reduce_fusion.4
  121.3 3.3 multiply_convert_fusion.2
  124.6 1.3 bitcast_select_fusion.7
  125.9 1.3 pad_maximum_fusion.1
  127.2 2.7 all-gather.2.cloned.1.call-done
  129.8 4.5 %fusion.40 = (bf16[32,24,768]{2,1,0:T(8,128)(2,1)S(1)}, bf16[32,24,768]{2,1,0:T(8,128)(2,1)}, bf16[32,24,768]{2,1,0:T(8,128)(2,1)}, bf16[32,24,768]{2,1,0:T(8,128)(2,1)}, bf16[32,24,768]{2,1,0:T(8,128)(2,1)S(1)}) fusion(bf16[32,216,768]{2,1,0:T(8,128)(2,1)} %bitcast.254), kind=kLoop, calls=%fused_computation.185 | loop fusion | bytes 11796480 | tf_op jit(solution)/shard_map/slice | solution.py:596
  134.4 3.1 slice.218
  138.1 1.6 fusion.46
  140.2 16.6 %add_convert_fusion = (bf16[1024,3072]{1,0:T(8,128)(2,1)}, bf16[1024,3072]{1,0:T(8,128)(2,1)}) fusion(f32[3072]{0:T(1024)S(1)} %add.246, bf16[768,768]{1,0:T(8,128)(2,1)} %bitcast.287, bf16[768,768]{1,0:T(8,128)(2,1)} %bitcast.289, bf16[768,768]{1,0:T(8,128)(2,1)} %bitcast.291, bf16[768,768]{1,0:T(8,128)(2,1)S(1)} %bitcast.285, ...), kind=kOutput, calls=%fused_computation.2 | convolution fusion | flops 4904976384 | bytes 20473856 | tf_op jit(solution)/shard_map/dot_general | solution.py:646
  156.8 7.2 %convert_reduce_fusion = (f32[3072]{0:T(1024)S(1)}, bf16[1024,3072]{1,0:T(8,128)(2,1)S(1)}) fusion(bf16[1024,3072]{1,0:T(8,128)(2,1)} %get-tuple-element.41, bf16[1024,768]{1,0:T(8,128)(2,1)S(1)} %bitcast.279, bf16[3072,768]{1,0:T(8,128)(2,1)S(1)} %bitcast.265), kind=kOutput, calls=%fused_computation | convolution fusion | flops 4847563776 | bytes 18886656 | tf_op jit(solution)/shard_map/dot_general | solution.py:28
  164.1 6.3 %convolution_convert_fusion.1 = bf16[768,3072]{1,0:T(8,128)(2,1)S(1)} fusion(bf16[1024,3072]{1,0:T(8,128)(2,1)S(1)} %get-tuple-element.42, f32[1024,768]{1,0:T(8,128)S(1)} %get-tuple-element.131, f32[768]{0:T(1024)S(1)} %add.243, f32[768]{0:T(1024)S(1)} %mul.289, f32[1024]{0:T(1024)S(1)} %fusion.28, f32[1024]{0:T(1024)S(1)} %broadcast_multiply_fusion.2), kind=kOutput, calls=%fused_computation.17 | convolution fusion | flops 4838129664 | bytes 14170112 | tf_op jit(solution)/shard_map/dot_general | solution.py:24
  171.3 1.3 slice-done.2
  173.8 5.9 %convolution_convert_fusion = bf16[3072,768]{1,0:T(8,128)(2,1)S(1)} fusion(bf16[1024,3072]{1,0:T(8,128)(2,1)S(1)} %bitcast.323, bf16[1024,768]{1,0:T(8,128)(2,1)S(1)} %copy-done.20), kind=kOutput, calls=%fused_computation.16 | convolution fusion | flops 4834197504 | bytes 12582912 | tf_op jit(solution)/shard_map/dot_general | solution.py:24
  181.4 12.0 %multiply_reduce_fusion.1 = (f32[768]{0:T(1024)S(1)}, f32[1024]{0:T(1024)S(1)}, f32[768]{0:T(1024)S(1)}, f32[1024,768]{1,0:T(8,128)S(1)}) fusion(f32[1024,768]{1,0:T(8,128)S(1)} %get-tuple-element.131, f32[1024]{0:T(1024)S(1)} %fusion.28, f32[1024]{0:T(1024)S(1)} %broadcast_multiply_fusion.2, f32[768]{0:T(1024)S(1)} %mul.289, ...), kind=kOutput, calls=%fused_computation.47 | convolution fusion | flops 4857000960 | bytes 17323008 | tf_op jit(solution)/shard_map/dot_general | solution.py:28
  193.4 2.6 fusion.39
  196.0 3.2 convert_reduce_fusion.5
  199.3 1.4 convolution_convert_fusion.4
  202.0 1.5 convolution_convert_fusion.5
  205.0 5.1 %multiply_convert_fusion.4 = bf16[1024,768]{1,0:T(8,128)(2,1)S(1)} fusion(f32[1024,768]{1,0:T(8,128)S(1)} %copy-done.8, bf16[1024,3072]{1,0:T(8,128)(2,1)S(1)} %bitcast.325, bf16[3072,768]{1,0:T(8,128)(2,1)S(1)} %bitcast.268, f32[1024]{0:T(1024)S(1)} %bitcast.300, f32[768]{0:T(1024)S(1)} %add.255), kind=kOutput, calls=%fused_computation.54 | convolution fusion | flops 4835770368 | bytes 15735808 | tf_op jit(solution)/shard_map/dot_general | solution.py:649
  213.7 2.3 add_convert_fusion.4
  216.0 1.7 broadcast_select_fusion.1
  217.7 1.3 pad_maximum_fusion.4
  219.1 52.7 %attend_backward.1 = bf16[2048,1152]{1,0:T(8,128)(2,1)} custom-call(s32[2,8]{1,0:T(2,128)} %get-tuple-element.136.bounds_ref, bf16[2048,1152]{1,0:T(8,128)(2,1)} %add_convert_fusion.1.packed_ref, bf16[2048,384]{1,0:T(8,128)(2,1)} %get-tuple-element.38.o_ref, bf16[2048,384]{1,0:T(8,128)(2,1)} %bitcast.256, s32[1,2048]{1,0:T(1,128)} %bitcast.312, ...), custom_call_target="tpu_custom_call" | custom-call | flops 12582912 | bytes 2359296 | tf_op jit(solution)/shard_map/attend_backward/pallas_call | solution.py:234
  271.7 7.5 %convolution_convert_fusion.2 = bf16[2048,768]{1,0:T(8,128)(2,1)S(1)} fusion(bf16[2048,1152]{1,0:T(8,128)(2,1)} %attend_backward.1, bf16[768,1152]{1,0:T(8,128)(2,1)} %bitcast.320), kind=kOutput, calls=%fused_computation.22 | convolution fusion | flops 3625451520 | bytes 9633792 | tf_op jit(solution)/shard_map/dot_general | solution.py:28
  279.2 1.4 dynamic-slice_bitcast_fusion
  282.2 1.7 fusion.25
  283.9 1.3 pad_maximum_fusion.2
  285.1 8.2 %convolution_convert_fusion.3 = bf16[768,1152]{1,0:T(8,128)(2,1)} fusion(bf16[2048,768]{1,0:T(8,128)(2,1)S(1)} %copy-done.15, bf16[2048,1152]{1,0:T(8,128)(2,1)} %attend_backward.1), kind=kOutput, calls=%fused_computation.23 | convolution fusion | flops 3624763392 | bytes 9633792 | tf_op jit(solution)/shard_map/dot_general | solution.py:24
  293.4 2.8 fusion.17
  296.2 1.6 fusion.16
  298.5 2.3 fusion.8
  303.3 56.0 %reduce_last.1 = (f32[24,1152]{1,0:T(8,128)}, f32[24,1152]{1,0:T(8,128)}, f32[24,384]{1,0:T(8,128)}, f32[24,384]{1,0:T(8,128)}, f32[8,128]{1,0:T(8,128)}) custom-call(bf16[4,2,2,48,1152]{4,3,2,1,0:T(8,128)(2,1)} %bitcast.276, bf16[4,2,2,48,384]{4,3,2,1,0:T(8,128)(2,1)} %bitcast.275, f32[4,2,2,16,128]{4,3,2,1,0:T(8,128)} %bitcast.293), custom_call_target="tpu_custom_call" | custom-call | tf_op jit(solution)/shard_map/reduce_last/pallas_call | solution.py:469
  361.7 1.4 slice_bitcast_fusion
  365.7 1.3 fusion.21
  367.0 1.3 pad_maximum_fusion.5
  369.9 1.6 slice.236
  (201 shorter events, 30.9 us)
Async XLA Ops:
  7.2 122.7 %all-gather.2.cloned.1.call-start = ((), (), s32[]{:S(2)}) async-start(), calls=%async_computation.1 | async-start | bytes 10948608 | tf_op jit(solution)/shard_map/all_gather | solution.py:510
  9.0 359.3 %reduce-scatter.2.cloned.1.call-start = ((), (), s32[]{:S(2)}) async-start(), calls=%async_computation.2 | async-start | bytes 9732096 | tf_op jit(solution)/shard_map/reduce_scatter | solution.py:514
  64.5 7.3 %copy-start = (bf16[2,2,512,768]{3,2,1,0:T(8,128)(2,1)S(1)}, bf16[2,2,512,768]{3,2,1,0:T(8,128)(2,1)}, u32[]{:S(2)}) copy-start(bf16[2,2,512,768]{3,2,1,0:T(8,128)(2,1)} %get-tuple-element.32) | copy-start | bytes 9437188
  72.9 1.5 copy-start.34
  74.4 5.8 %copy-start.33 = (s32[2,1,4]{2,1,0:T(1,128)S(1)}, s32[2,1,4]{2,1,0:T(1,128)}, u32[]{:S(2)}) copy-start(s32[2,1,4]{2,1,0:T(1,128)} %param.17) | copy-start | bytes 100
  80.2 35.0 %collective-permute-start = (bf16[512,768]{1,0:T(8,128)(2,1)}, bf16[512,768]{1,0:T(8,128)(2,1)}, u32[]{:S(2)}, u32[]{:S(2)}) collective-permute-start(bf16[512,768]{1,0:T(8,128)(2,1)} %dynamic-slice_bitcast_fusion.4), channel_id=1, source_target_pairs={{0,2},{1,3},{2,0},{3,1},{4,6},{5,7},{6,4},{7,5},{8,10},{9,11},{10,... | collective-permute-start | bytes 2359304 | tf_op jit(solution)/shard_map/ppermute | solution.py:629
  80.5 2.4 copy-start.31
  111.2 4.0 %copy-start.10 = (bf16[2048,384]{1,0:T(8,128)(2,1)S(1)}, bf16[2048,384]{1,0:T(8,128)(2,1)}, u32[]{:S(2)}) copy-start(bf16[2048,384]{1,0:T(8,128)(2,1)} %get-tuple-element.38.o_ref) | copy-start | bytes 4718596
  111.2 6.1 %copy-start.22 = (bf16[2,512,768]{2,1,0:T(8,128)(2,1)S(1)}, bf16[2,512,768]{2,1,0:T(8,128)(2,1)}, u32[]{:S(2)}) copy-start(bf16[2,512,768]{2,1,0:T(8,128)(2,1)} %param.16) | copy-start | bytes 4718596
  116.2 8.4 %collective-permute-start.1 = (bf16[2,512,384]{2,1,0:T(8,128)(2,1)}, bf16[2,512,384]{2,1,0:T(8,128)(2,1)}, u32[]{:S(2)}, u32[]{:S(2)}) collective-permute-start(bf16[2,512,384]{2,1,0:T(8,128)(2,1)} %dynamic-slice_bitcast_fusion.3), channel_id=1, source_target_pairs={{0,1},{1,0},{2,3},{3,2},{4,5},{5,4},{6,7},{7,6},{8,9},{9,8},{10,11... | collective-permute-start | bytes 2359304 | tf_op jit(solution)/shard_map/ppermute | solution.py:635
  118.6 2.6 copy-start.4
  121.3 3.3 copy-start.11
  134.4 3.1 copy-start.26
  134.4 3.3 copy-start.18
  134.4 3.7 copy-start.25
  137.5 19.3 %copy-start.14 = (bf16[32,96,768]{2,1,0:T(8,128)(2,1)}, bf16[32,96,768]{2,1,0:T(8,128)(2,1)S(1)}, u32[]{:S(2)}) copy-start(bf16[32,96,768]{2,1,0:T(8,128)(2,1)S(1)} %slice.218) | copy-start | bytes 14155780
  139.7 53.7 %copy-start.7 = (f32[1024,768]{1,0:T(8,128)}, f32[1024,768]{1,0:T(8,128)S(1)}, u32[]{:S(2)}) copy-start(f32[1024,768]{1,0:T(8,128)S(1)} %get-tuple-element.131) | copy-start | bytes 9437188
  140.2 16.6 %copy-start.21 = (bf16[2,512,768]{2,1,0:T(8,128)(2,1)S(1)}, bf16[2,512,768]{2,1,0:T(8,128)(2,1)}, u32[]{:S(2)}) copy-start(bf16[2,512,768]{2,1,0:T(8,128)(2,1)} %get-tuple-element.63) | copy-start | bytes 4718596
  164.0 6.3 %copy-start.35 = (bf16[1024,3072]{1,0:T(8,128)(2,1)}, bf16[1024,3072]{1,0:T(8,128)(2,1)S(1)}, u32[]{:S(2)}) copy-start(bf16[1024,3072]{1,0:T(8,128)(2,1)S(1)} %get-tuple-element.42) | copy-start | bytes 18874372
  170.4 2.2 slice-start.2
  170.7 2.6 slice-start.3
  170.9 2.9 copy-start.20
  179.7 1.3 copy-start.28
  179.7 1.6 copy-start.29
  181.4 12.0 %copy-start.9 = (bf16[32,192,768]{2,1,0:T(8,128)(2,1)}, bf16[32,192,768]{2,1,0:T(8,128)(2,1)S(1)}, u32[]{:S(2)}) copy-start(bf16[32,192,768]{2,1,0:T(8,128)(2,1)S(1)} %constant_dynamic-update-slice_fusion) | copy-start | bytes 28311556
  196.0 3.2 copy-start.27
  196.0 8.9 %slice-start = ((s8[4718592]{0:T(1024)(128)(4,1)}), s8[4194304]{0:T(1024)(128)(4,1)S(1)}, s32[]{:S(2)}) async-start(s8[4718592]{0:T(1024)(128)(4,1)} %bitcast.266), calls=%async_computation.3 | async-start | bytes 8388608
  196.0 8.9 %slice-start.4 = ((s8[6291456]{0:T(1024)(128)(4,1)}), s8[4194304]{0:T(1024)(128)(4,1)S(1)}, s32[]{:S(2)}) async-start(s8[6291456]{0:T(1024)(128)(4,1)} %bitcast.324), calls=%async_computation.7 | async-start | bytes 8388608
  199.2 2.7 copy-start.19
  199.3 5.7 %slice-start.1 = ((s8[4718592]{0:T(1024)(128)(4,1)}), s8[524288]{0:T(1024)(128)(4,1)S(1)}, s32[]{:S(2)}) async-start(s8[4718592]{0:T(1024)(128)(4,1)} %bitcast.266), calls=%async_computation.4 | async-start | bytes 1048576
  199.3 5.7 %slice-start.5 = ((s8[6291456]{0:T(1024)(128)(4,1)}), s8[2097152]{0:T(1024)(128)(4,1)S(1)}, s32[]{:S(2)}) async-start(s8[6291456]{0:T(1024)(128)(4,1)} %bitcast.324), calls=%async_computation.8 | async-start | bytes 4194304
  200.7 2.7 copy-start.24
  201.7 3.2 copy-start.8
  201.7 14.3 %collective-permute-start.3 = (bf16[1024,384]{1,0:T(8,128)(2,1)}, bf16[1024,384]{1,0:T(8,128)(2,1)}, u32[]{:S(2)}, u32[]{:S(2)}) collective-permute-start(bf16[1024,384]{1,0:T(8,128)(2,1)} %constant_dynamic-slice_fusion.1), channel_id=1, source_target_pairs={{0,1},{1,0},{2,3},{3,2},{4,5},{5,4},{6,7},{7,6},{8,9},{9,8},{10,11... | collective-permute-start | bytes 2359304 | tf_op jit(solution)/shard_map/ppermute | solution.py:677
  203.4 1.2 copy-start.30
  204.7 9.0 %collective-permute-start.6 = (bf16[768,384]{1,0:T(8,128)(2,1)}, bf16[768,384]{1,0:T(8,128)(2,1)}, u32[]{:S(2)}, u32[]{:S(2)}) collective-permute-start(bf16[768,384]{1,0:T(8,128)(2,1)} %constant_dynamic-slice_fusion), channel_id=1, source_target_pairs={{0,1},{1,0},{2,3},{3,2},{4,5},{5,4},{6,7},{7,6},{8,9},{9,8},{10,11... | collective-permute-start | bytes 1769480 | tf_op jit(solution)/shard_map/ppermute | solution.py:705
  212.2 69.9 %collective-permute-start.2 = (bf16[512,768]{1,0:T(8,128)(2,1)}, bf16[512,768]{1,0:T(8,128)(2,1)}, u32[]{:S(2)}, u32[]{:S(2)}) collective-permute-start(bf16[512,768]{1,0:T(8,128)(2,1)} %dynamic-slice_bitcast_fusion.2), channel_id=1, source_target_pairs={{0,2},{1,3},{2,0},{3,1},{4,6},{5,7},{6,4},{7,5},{8,10},{9,11},{10,... | collective-permute-start | bytes 2359304 | tf_op jit(solution)/shard_map/ppermute | solution.py:559
  271.7 9.4 %copy-start.6 = (bf16[2048,1152]{1,0:T(8,128)(2,1)S(1)}, bf16[2048,1152]{1,0:T(8,128)(2,1)}, u32[]{:S(2)}) copy-start(bf16[2048,1152]{1,0:T(8,128)(2,1)} %attend_backward.1) | copy-start | bytes 14155780
  279.2 2.6 copy-start.16
  280.6 12.8 %collective-permute-start.4 = (bf16[2,512,768]{2,1,0:T(8,128)(2,1)}, bf16[2,512,768]{2,1,0:T(8,128)(2,1)}, u32[]{:S(2)}, u32[]{:S(2)}) collective-permute-start(bf16[2,512,768]{2,1,0:T(8,128)(2,1)} %dynamic-slice_bitcast_fusion), channel_id=1, source_target_pairs={{0,1},{1,0},{2,3},{3,2},{4,5},{5,4},{6,7},{7,6},{8,9},{9,8},{10,11... | collective-permute-start | bytes 4718600 | tf_op jit(solution)/shard_map/ppermute | solution.py:685
  282.1 3.0 copy-start.15
  285.1 8.2 %copy-start.17 = (bf16[2048,768]{1,0:T(8,128)(2,1)S(1)}, bf16[2048,768]{1,0:T(8,128)(2,1)}, u32[]{:S(2)}) copy-start(bf16[2048,768]{1,0:T(8,128)(2,1)} %copy-done.16) | copy-start | bytes 9437188
  296.1 1.9 copy-start.1
  296.2 2.1 copy-start.3
  296.2 2.3 copy-start.5
  302.0 63.7 %copy-start.13 = (bf16[1024,768]{1,0:T(8,128)(2,1)S(1)}, bf16[1024,768]{1,0:T(8,128)(2,1)}, u32[]{:S(2)}) copy-start(bf16[1024,768]{1,0:T(8,128)(2,1)} %copy-done.12) | copy-start | bytes 4718596
  302.0 63.7 %collective-permute-start.5 = (bf16[512,768]{1,0:T(8,128)(2,1)S(1)}, bf16[512,768]{1,0:T(8,128)(2,1)}, u32[]{:S(2)}, u32[]{:S(2)}) collective-permute-start(bf16[512,768]{1,0:T(8,128)(2,1)S(1)} %dynamic-slice_bitcast_fusion.1), channel_id=1, source_target_pairs={{0,2},{1,3},{2,0},{3,1},{4,6},{5,7},{6,4},{7,5},{8,10},{9,11},{10,... | collective-permute-start | bytes 2359304 | tf_op jit(solution)/shard_map/ppermute | solution.py:559
  365.6 2.6 copy-start.32
  (3 other events, 3.2 us)
Sparse Core Ops, SparseCore 0:
  10.9 118.8 all-gather.1
  196.1 135.0 reduce-scatter.1
where the time goes:
time: 382 us; the launch traced here: 379 us
  Pallas kernels  192 us (50%)
  matrix products  79.1 us (21%)
  other arithmetic  45.6 us (12%)
  local copies, waits for them, and re-layouts  38.3 us (10%)
  between operations  15.4 us (4%)
  waiting for transfers between devices  4.27 us (1%)
    pallas_call x1, Pallas kernels, reduce_last(): pl.pallas_call(reduce_kernel, name='reduce_last', out_shape=(jax.ShapeDty...  56 us
    pallas_call x1, Pallas kernels, gather_first(): pl.pallas_call(gather_kernel, name='gather_first', out_shape=(jax.ShapeDt...  55.4 us
    pallas_call x1, Pallas kernels, attend_backward(): pl.pallas_call(attend_back_kernel, name='attend_backward', out_shape=jax....  52.7 us
    dot_general x4, matrix products, against_rows(): lax.dot_general(first, second, (((1,), (1,)), ((), ())), preferred_elemen...  28.1 us
    pallas_call x1, Pallas kernels, attend_forward(): pl.pallas_call(attend_kernel, name='attend_forward', out_shape=(jax.Shape...  26.4 us
    dot_general x4, matrix products, outer_sum(): lax.dot_general(first, second, (((0,), (0,)), ((), ())), preferred_elemen...  21.9 us
    dot_general x1, matrix products, local(): jnp.dot(normed_two_low, full_expand, preferred_element_type=F32)  16.6 us
    unnamed x106, local copies, waits for them, and re-layouts  9.08 us
  transfers between devices with their start and end apart: 9, of which 2 were waited for; matrix products, arithmetic and copies ran while one was open for 24% of the time, Pallas kernels for 50%

commit v1 on v0

--- a/solution.py
+++ b/solution.py
@@ -388,34 +388,28 @@
     streams = []
     for i, source in enumerate((big_ref, flat_ref, tiny_ref)):
         streams.append((source,) + scratch[10 * i : 10 * i + 10])
-    first_twin = device(z, x + (1 - core) * (1 - 2 * x), y + core * (1 - 2 * y), core)
-    second_twin = device(z, x + core * (1 - 2 * x), y + (1 - core) * (1 - 2 * y), core)
-    keep = (1 - core) * y + core * x
+    first_twin, second_twin = device(z, 1 - x, y, core), device(z, x, 1 - y, core)
     order = (1, 2, 3, 0)
     one, two, three = {}, {}, {}
     for t in order:
         k = lax.rem(z + t, 4)
         for j in (0, 1):
-            ix = (1 - core) * (1 - x) + core * j
-            iy = (1 - core) * j + core * (1 - y)
             for i, (source, came_one, *_, leave, arrive) in enumerate(streams):
-                one[t, j, i] = send(source.at[k, ix, iy], came_one.at[t, j], (leave, arrive), 2 * t + j, first_twin)
+                one[t, j, i] = send(source.at[k, 1 - x, j], came_one.at[t, j], (leave, arrive), 2 * t + j, first_twin)
     for t in order:
         k = lax.rem(z + t, 4)
         for i, (source, came_one, sum_one, came_two, *_, leave, arrive) in enumerate(streams):
             for j in (0, 1):
                 one[t, j, i].wait_recv()
-                ix = (1 - core) * x + core * j
-                iy = (1 - core) * j + core * y
-                total = source[k, ix, iy].astype(F32) + came_one[t, j].astype(F32)
+                total = source[k, x, j].astype(F32) + came_one[t, j].astype(F32)
                 sum_one[t, j] = total.astype(sum_one.dtype)
-            two[t, i] = send(sum_one.at[t, 1 - keep], came_two.at[t], (leave, arrive), 8 + t, second_twin)
+            two[t, i] = send(sum_one.at[t, 1 - y], came_two.at[t], (leave, arrive), 8 + t, second_twin)
     for t in order:
         for i, (_, _, sum_one, came_two, sum_two, came_three, total_ref, _, leave, arrive) in enumerate(
             [(s[0], s[1], s[2], s[3], s[4], s[5], s[6], s[7], s[9], s[10]) for s in streams]
         ):
             two[t, i].wait_recv()
-            total = sum_one[t, keep].astype(F32) + came_two[t].astype(F32)
+            total = sum_one[t, y].astype(F32) + came_two[t].astype(F32)
             if t == 0:
                 total_ref[...] = total
             else:
@@ -548,7 +542,7 @@
 
     def placed(both, came):
         kept = lax.dynamic_index_in_dim(both, mine, 0, keepdims=False)
-        return jnp.stack([jnp.where(mine == 0, kept, came), jnp.where(mine == 0, came, kept)])
+        return jnp.where((jnp.arange(micro_count) == mine)[:, None, None], kept[None], came[None])
 
     def own_micro(both):
         return placed(both, lax.ppermute(swap_of(both), "seq", swap_micro))
@@ -557,11 +551,11 @@
         kept = lax.dynamic_index_in_dim(blocks, mine, 0, keepdims=False)
         sent = lax.dynamic_index_in_dim(blocks, 1 - mine, 0, keepdims=False)
         came = lax.ppermute(sent, "seq", swap_micro)
-        return jnp.stack([jnp.where(mine == 0, kept, came), jnp.where(mine == 0, came, kept)])
+        return jnp.where((jnp.arange(micro_count) == mine)[:, None, None], kept[None], came[None])
 
     def interleave(own, other):
-        first, second = jnp.where(core == 0, own, other), jnp.where(core == 0, other, own)
-        return jnp.stack([first, second], axis=1).reshape((bucket,) + own.shape[2:])
+        here = (jnp.arange(share) == core)[None, :, None, None]
+        return jnp.where(here, own[:, None], other[:, None]).reshape((bucket,) + own.shape[2:])
 
 
     vectors = (gain_first, shift_first, packed_bias, output_bias, gain_second, shift_second, expand_bias, reduce_bias)

time: 382 us -> 393 us (1.029)
  Pallas kernels: 192 us -> 180 us
  starting transfers between devices: 3.67 us -> 12.2 us
  local copies, waits for them, and re-layouts: 38.3 us -> 46 us
  matrix products: 79.1 us -> 85.1 us
    pallas_call x1, Pallas kernels: 56 us -> 44 us  [reduce_last(): pl.pallas_call(reduce_kernel, name='reduce_last', out_shape=(jax.ShapeDty...]
    ppermute x2, starting transfers between devices: 1.44 us -> 10.5 us  [home_micro(): came = lax.ppermute(sent, 'seq', swap_micro)]
    another operation x7 -> x2, other arithmetic: 8.31 us -> 0.76 us  [the longest x1 0.58 us: local(): high_blocks = jnp.stack([high, jnp.clip(free, block_ids + 1, high)])]
    select_n x1 -> x3, other arithmetic: 1.75 us -> 8.19 us  [the longest x1 3.21 us: home_micro(): jnp.where((jnp.arange(micro_count) == mine)[:, None, None], kept[None], c...]
    broadcast_in_dim x0 -> x7, local copies, waits for them, and re-layouts: none -> 5.67 us  [the longest x4 2.93 us: home_micro(): jnp.where((jnp.arange(micro_count) == mine)[:, None, None], kept[None], c...]
    unnamed x106 -> x96, local copies, waits for them, and re-layouts: 9.08 us -> 11.2 us
  transfers between devices with their start and end apart: 9 -> 9, of which waited for: 2 -> 1; matrix products, arithmetic and copies ran while one was open for 24% -> 25% of each run, Pallas kernels for 50% -> 46%
where the time goes in v1:
time: 393 us; the launch traced here: 386 us
  Pallas kernels  180 us (46%)
  matrix products  85.1 us (22%)
  local copies, waits for them, and re-layouts  46 us (12%)
  other arithmetic  42.7 us (11%)
  between operations  15.3 us (4%)
  starting transfers between devices  12.2 us (3%)
  waiting for transfers between devices  4.25 us (1%)
    pallas_call x1, Pallas kernels, gather_first(): pl.pallas_call(gather_kernel, name='gather_first', out_shape=(jax.ShapeDt...  55.4 us
    pallas_call x1, Pallas kernels, attend_backward(): pl.pallas_call(attend_back_kernel, name='attend_backward', out_shape=jax....  52.6 us
    pallas_call x1, Pallas kernels, reduce_last(): pl.pallas_call(reduce_kernel, name='reduce_last', out_shape=(jax.ShapeDty...  44 us
    dot_general x4, matrix products, against_rows(): lax.dot_general(first, second, (((1,), (1,)), ((), ())), preferred_elemen...  29.4 us
    pallas_call x1, Pallas kernels, attend_forward(): pl.pallas_call(attend_kernel, name='attend_forward', out_shape=(jax.Shape...  26.5 us
    dot_general x4, matrix products, outer_sum(): lax.dot_general(first, second, (((0,), (0,)), ((), ())), preferred_elemen...  25.1 us
    dot_general x1, matrix products, local(): jnp.dot(normed_two_low, full_expand, preferred_element_type=F32)  16.5 us
    unnamed x96, local copies, waits for them, and re-layouts  11.2 us
  transfers between devices with their start and end apart: 9, of which 1 were waited for; matrix products, arithmetic and copies ran while one was open for 25% of the time, Pallas kernels for 46%

profile of v1, /device:TPU:9, one launch (start us, length us, event | category | flops | bytes accessed | tf_op | source)
XLA Modules:
  0.0 385.8 jit_solution(7499087138895365613)
XLA Ops:
  7.2 1.8 pack_second.1
  9.1 55.4 %gather_first.1 = (bf16[2,2,512,768]{3,2,1,0:T(8,128)(2,1)}, bf16[4,2,2,2,24,1152]{5,4,3,2,1,0:T(8,128)(2,1)}, f32[4,2,2,2,8,128]{5,4,3,2,1,0:T(8,128)}) custom-call(bf16[2,512,768]{2,1,0:T(8,128)(2,1)} %token_ref.1, bf16[24,2304]{1,0:T(8,128)(2,1)} %weight_ref.1, bf16[24]{0:T(256)(128)(2,1)} %rest_0_.1, bf16[24]{0:T(256)(128)(2,1)} %rest_1_.1, ...), custom_call_target="tpu_custom_call" | custom-call | tf_op jit(solution)/shard_map/gather_first/pallas_call | solution.py:370
  65.7 1.4 fusion.40
  67.4 2.6 dynamic-slice_bitcast_fusion.3
  71.7 1.5 add_convert_fusion.2
  73.2 6.0 %add_convert_fusion.1.packed_ref = bf16[2048,1152]{1,0:T(8,128)(2,1)} fusion(bf16[2048,768]{1,0:T(8,128)(2,1)S(1)} %bitcast.232, bf16[768,1152]{1,0:T(8,128)(2,1)S(1)} %bitcast.281, f32[1152]{0:T(1024)S(1)} %pad_maximum_fusion.7), kind=kOutput, calls=%fused_computation.7 | convolution fusion | flops 3628597248 | bytes 9638400 | tf_op jit(solution)/shard_map/dot_general | solution.py:619
  83.2 1.3 constant_dynamic-slice_fusion.5
  84.5 26.5 %attend_forward.1 = (bf16[2048,384]{1,0:T(8,128)(2,1)}, f32[6,2048]{1,0:T(8,128)}) custom-call(s32[2,8]{1,0:T(2,128)} %pad_add_fusion.bounds_ref, bf16[2048,1152]{1,0:T(8,128)(2,1)} %add_convert_fusion.1.packed_ref, s32[1,2048]{1,0:T(1,128)} %bitcast.271), custom_call_target="tpu_custom_call" | custom-call | flops 3221225472 | bytes 7077888 | tf_op jit(solution)/shard_map/attend_forward/pallas_call | solution.py:129
  111.0 4.2 %collective-permute-done = bf16[512,768]{1,0:T(8,128)(2,1)} collective-permute-done((bf16[512,768]{1,0:T(8,128)(2,1)}, bf16[512,768]{1,0:T(8,128)(2,1)}, u32[]{:S(2)}, u32[]{:S(2)}) %collective-permute-start) | collective-permute-done | bytes 786464 | tf_op jit(solution)/shard_map/ppermute | solution.py:623
  115.2 2.2 dynamic-slice_bitcast_fusion.6
  117.4 1.2 collective-permute-start.1
  118.6 2.5 fusion.5
  121.1 2.6 bitcast_select_fusion.1
  123.7 3.0 convert_reduce_fusion.4
  126.7 1.5 bitcast_select_fusion.3
  128.3 1.3 pad_maximum_fusion.1
  129.5 2.6 slice.218
  132.2 6.4 %fusion.37 = (bf16[32,24,768]{2,1,0:T(8,128)(2,1)S(1)}, bf16[32,24,768]{2,1,0:T(8,128)(2,1)}, bf16[32,24,768]{2,1,0:T(8,128)(2,1)}, bf16[32,24,768]{2,1,0:T(8,128)(2,1)}, bf16[32,24,768]{2,1,0:T(8,128)(2,1)S(1)}) fusion(bf16[32,216,768]{2,1,0:T(8,128)(2,1)} %bitcast.219), kind=kLoop, calls=%fused_computation.180 | loop fusion | bytes 11796480 | tf_op jit(solution)/shard_map/slice | solution.py:590
  138.6 1.6 fusion.43
  140.7 16.5 %add_convert_fusion = (bf16[1024,3072]{1,0:T(8,128)(2,1)}, bf16[1024,3072]{1,0:T(8,128)(2,1)}) fusion(f32[3072]{0:T(1024)S(1)} %add.246, bf16[768,768]{1,0:T(8,128)(2,1)} %bitcast.247, bf16[768,768]{1,0:T(8,128)(2,1)} %bitcast.249, bf16[768,768]{1,0:T(8,128)(2,1)} %bitcast.251, bf16[768,768]{1,0:T(8,128)(2,1)S(1)} %bitcast.245, ...), kind=kOutput, calls=%fused_computation.2 | convolution fusion | flops 4904976384 | bytes 20473856 | tf_op jit(solution)/shard_map/dot_general | solution.py:640
  157.3 7.2 %convert_reduce_fusion = (f32[3072]{0:T(1024)S(1)}, bf16[1024,3072]{1,0:T(8,128)(2,1)S(1)}) fusion(bf16[1024,3072]{1,0:T(8,128)(2,1)} %get-tuple-element.41, bf16[1024,768]{1,0:T(8,128)(2,1)S(1)} %bitcast.241, bf16[3072,768]{1,0:T(8,128)(2,1)S(1)} %bitcast.227), kind=kOutput, calls=%fused_computation | convolution fusion | flops 4847563776 | bytes 18886656 | tf_op jit(solution)/shard_map/dot_general | solution.py:28
  164.5 6.3 %convolution_convert_fusion.1 = bf16[768,3072]{1,0:T(8,128)(2,1)S(1)} fusion(bf16[1024,3072]{1,0:T(8,128)(2,1)S(1)} %get-tuple-element.42, f32[1024,768]{1,0:T(8,128)S(1)} %get-tuple-element.133, f32[768]{0:T(1024)S(1)} %add.243, f32[768]{0:T(1024)S(1)} %mul.289, f32[1024]{0:T(1024)S(1)} %fusion.24, f32[1024]{0:T(1024)S(1)} %broadcast_multiply_fusion.2), kind=kOutput, calls=%fused_computation.17 | convolution fusion | flops 4838129664 | bytes 14170112 | tf_op jit(solution)/shard_map/dot_general | solution.py:24
  171.8 1.3 slice-done.2
  174.3 6.3 %convolution_convert_fusion = bf16[3072,768]{1,0:T(8,128)(2,1)S(1)} fusion(bf16[1024,3072]{1,0:T(8,128)(2,1)S(1)} %bitcast.283, bf16[1024,768]{1,0:T(8,128)(2,1)S(1)} %copy-done.4, f32[1024]{0:T(1024)S(1)} %bitcast.264), kind=kOutput, calls=%fused_computation.16 | convolution fusion | flops 4837343232 | bytes 12587008 | tf_op jit(solution)/shard_map/dot_general | solution.py:24
  182.6 13.3 %multiply_reduce_fusion.1 = (f32[768]{0:T(1024)S(1)}, f32[1024]{0:T(1024)S(1)}, f32[768]{0:T(1024)S(1)}, f32[1024,768]{1,0:T(8,128)}) fusion(f32[1024,768]{1,0:T(8,128)S(1)} %get-tuple-element.133, f32[1024]{0:T(1024)S(1)} %fusion.24, f32[1024]{0:T(1024)S(1)} %broadcast_multiply_fusion.2, f32[768]{0:T(1024)S(1)} %mul.289, ...), kind=kOutput, calls=%fused_computation.46 | convolution fusion | flops 4857000960 | bytes 17323008 | tf_op jit(solution)/shard_map/dot_general | solution.py:28
  196.0 3.6 fusion.36
  201.3 1.2 copy-done.18
  202.5 1.4 convolution_convert_fusion.4
  203.9 1.4 constant_dynamic-slice_fusion.2
  208.2 6.3 %multiply_convert_fusion.4 = bf16[1024,768]{1,0:T(8,128)(2,1)} fusion(f32[1024,768]{1,0:T(8,128)S(1)} %copy-done.7, bf16[1024,3072]{1,0:T(8,128)(2,1)S(1)} %bitcast.285, bf16[3072,768]{1,0:T(8,128)(2,1)S(1)} %bitcast.230, f32[1024]{0:T(1024)S(1)} %bitcast.266, f32[768]{0:T(1024)S(1)} %add.255), kind=kOutput, calls=%fused_computation.54 | convolution fusion | flops 4835770368 | bytes 15735808 | tf_op jit(solution)/shard_map/dot_general | solution.py:643
  214.6 2.7 dynamic-slice_bitcast_fusion.5
  217.3 2.0 collective-permute-start.2
  219.5 3.5 convolution_convert_fusion.5
  224.4 2.4 bitcast_select_fusion.go_ref
  226.8 52.6 %attend_backward.1 = bf16[2048,1152]{1,0:T(8,128)(2,1)} custom-call(s32[2,8]{1,0:T(2,128)} %pad_add_fusion.1.bounds_ref, bf16[2048,1152]{1,0:T(8,128)(2,1)} %add_convert_fusion.1.packed_ref, bf16[2048,384]{1,0:T(8,128)(2,1)} %get-tuple-element.38.o_ref, bf16[2048,384]{1,0:T(8,128)(2,1)} %bitcast_select_fusion.go_ref, s32[1,2048]{1,0:T(1,128)} %bitcast.272, ...), custom_call_target="tpu_custom_call" | custom-call | flops 12582912 | bytes 2359296 | tf_op jit(solution)/shard_map/attend_backward/pallas_call | solution.py:234
  279.4 7.5 %convolution_convert_fusion.2 = bf16[2048,768]{1,0:T(8,128)(2,1)S(1)} fusion(bf16[2048,1152]{1,0:T(8,128)(2,1)} %attend_backward.1, bf16[768,1152]{1,0:T(8,128)(2,1)} %bitcast.280), kind=kOutput, calls=%fused_computation.22 | convolution fusion | flops 3625451520 | bytes 9633792 | tf_op jit(solution)/shard_map/dot_general | solution.py:28
  286.9 1.3 dynamic-slice_bitcast_fusion
  288.2 3.6 add_convert_fusion.4
  292.8 9.0 %convolution_convert_fusion.3 = bf16[768,1152]{1,0:T(8,128)(2,1)} fusion(bf16[2048,768]{1,0:T(8,128)(2,1)} %fusion.5, bf16[2048,1152]{1,0:T(8,128)(2,1)} %attend_backward.1), kind=kOutput, calls=%fused_computation.23 | convolution fusion | flops 3624763392 | bytes 9633792 | tf_op jit(solution)/shard_map/dot_general | solution.py:24
  301.8 2.7 fusion.17
  304.6 1.6 copy-done.2
  306.2 1.9 fusion.16
  309.1 4.1 %fusion.8 = bf16[1024,768]{1,0:T(8,128)(2,1)S(1)} fusion(f32[2,512,768]{2,1,0:T(8,128)} %copy-done.2, f32[1024,768]{1,0:T(8,128)} %copy-done.1, bf16[1024,768]{1,0:T(8,128)(2,1)} %bitcast_select_fusion.1, f32[1024]{0:T(1024)S(1)} %bitcast.275, f32[1024]{0:T(1024)S(1)} %get-tuple-element.122, f32[1024]{0:T(1024)S(1)} %bitcast.273, ...), kind=kLoop, calls=%fused_computation.26 | loop fusion | flops 11010048 | bytes 11037700 | tf_op jit(solution)/shard_map/convert_element_type | solution.py:683
  313.4 8.5 %collective-permute-start.5 = (bf16[512,768]{1,0:T(8,128)(2,1)S(1)}, bf16[512,768]{1,0:T(8,128)(2,1)S(1)}, u32[]{:S(2)}, u32[]{:S(2)}) collective-permute-start(bf16[512,768]{1,0:T(8,128)(2,1)S(1)} %get-tuple-element.83), channel_id=1, source_target_pairs={{0,2},{1,3},{2,0},{3,1},{4,6},{5,7},{6,4},{7,5},{8,10},{9,11},{10,... | collective-permute-start | bytes 2359304 | tf_op jit(solution)/shard_map/ppermute | solution.py:553
  321.8 44.0 %reduce_last.1 = (f32[24,1152]{1,0:T(8,128)}, f32[24,1152]{1,0:T(8,128)}, f32[24,384]{1,0:T(8,128)}, f32[24,384]{1,0:T(8,128)}, f32[8,128]{1,0:T(8,128)}) custom-call(bf16[4,2,2,48,1152]{4,3,2,1,0:T(8,128)(2,1)} %bitcast.237, bf16[4,2,2,48,384]{4,3,2,1,0:T(8,128)(2,1)} %bitcast.236, f32[4,2,2,16,128]{4,3,2,1,0:T(8,128)} %bitcast.253), custom_call_target="tpu_custom_call" | custom-call | tf_op jit(solution)/shard_map/reduce_last/pallas_call | solution.py:463
  368.3 1.4 slice_bitcast_fusion
  372.2 3.2 broadcast_select_fusion
  377.0 1.6 slice.236
  (193 shorter events, 26.3 us)
Async XLA Ops:
  7.2 122.4 %all-gather.2.cloned.1.call-start = ((), (), s32[]{:S(2)}) async-start(), calls=%async_computation.1 | async-start | bytes 10948608 | tf_op jit(solution)/shard_map/all_gather | solution.py:504
  9.0 366.4 %reduce-scatter.2.cloned.1.call-start = ((), (), s32[]{:S(2)}) async-start(), calls=%async_computation.2 | async-start | bytes 9732096 | tf_op jit(solution)/shard_map/reduce_scatter | solution.py:508
  64.5 5.5 %copy-start = (bf16[2,2,512,768]{3,2,1,0:T(8,128)(2,1)S(1)}, bf16[2,2,512,768]{3,2,1,0:T(8,128)(2,1)}, u32[]{:S(2)}) copy-start(bf16[2,2,512,768]{3,2,1,0:T(8,128)(2,1)} %get-tuple-element.32) | copy-start | bytes 9437188
  71.7 1.5 copy-start.29
  73.2 6.0 %copy-start.28 = (s32[2,1,4]{2,1,0:T(1,128)S(1)}, s32[2,1,4]{2,1,0:T(1,128)}, u32[]{:S(2)}) copy-start(s32[2,1,4]{2,1,0:T(1,128)} %param.17) | copy-start | bytes 100
  79.2 36.0 %collective-permute-start = (bf16[512,768]{1,0:T(8,128)(2,1)}, bf16[512,768]{1,0:T(8,128)(2,1)}, u32[]{:S(2)}, u32[]{:S(2)}) collective-permute-start(bf16[512,768]{1,0:T(8,128)(2,1)} %get-tuple-element.37), channel_id=1, source_target_pairs={{0,2},{1,3},{2,0},{3,1},{4,6},{5,7},{6,4},{7,5},{8,10},{9,11},{10,... | collective-permute-start | bytes 2359304 | tf_op jit(solution)/shard_map/ppermute | solution.py:623
  79.5 5.0 %copy-start.26 = (s32[2048]{0:T(1024)}, s32[2048]{0:T(1024)S(1)}, u32[]{:S(2)}) copy-start(s32[2048]{0:T(1024)S(1)} %get-tuple-element.61) | copy-start | bytes 24580
  117.4 9.4 %collective-permute-start.1 = (bf16[2,512,384]{2,1,0:T(8,128)(2,1)}, bf16[2,512,384]{2,1,0:T(8,128)(2,1)}, u32[]{:S(2)}, u32[]{:S(2)}) collective-permute-start(bf16[2,512,384]{2,1,0:T(8,128)(2,1)} %dynamic-slice_bitcast_fusion.6), channel_id=1, source_target_pairs={{0,1},{1,0},{2,3},{3,2},{4,5},{5,4},{6,7},{7,6},{8,9},{9,8},{10,11... | collective-permute-start | bytes 2359304 | tf_op jit(solution)/shard_map/ppermute | solution.py:629
  118.6 2.5 copy-start.9
  132.2 25.1 %copy-start.10 = (bf16[32,96,768]{2,1,0:T(8,128)(2,1)}, bf16[32,96,768]{2,1,0:T(8,128)(2,1)S(1)}, u32[]{:S(2)}) copy-start(bf16[32,96,768]{2,1,0:T(8,128)(2,1)S(1)} %slice.218) | copy-start | bytes 14155780
  132.2 6.4 %copy-start.15 = (bf16[2,512,768]{2,1,0:T(8,128)(2,1)S(1)}, bf16[2,512,768]{2,1,0:T(8,128)(2,1)}, u32[]{:S(2)}) copy-start(bf16[2,512,768]{2,1,0:T(8,128)(2,1)} %pad_maximum_fusion.1) | copy-start | bytes 4718596
  132.2 6.4 %copy-start.16 = (bf16[2,1,512,768]{3,2,1,0:T(8,128)(2,1)S(1)}, bf16[2,1,512,768]{3,2,1,0:T(8,128)(2,1)}, u32[]{:S(2)}) copy-start(bf16[2,1,512,768]{3,2,1,0:T(8,128)(2,1)} %constant_dynamic-slice_fusion.5) | copy-start | bytes 4718596
  138.6 1.6 copy-start.19
  140.2 40.8 %copy-start.6 = (f32[1024,768]{1,0:T(8,128)}, f32[1024,768]{1,0:T(8,128)S(1)}, u32[]{:S(2)}) copy-start(f32[1024,768]{1,0:T(8,128)S(1)} %get-tuple-element.133) | copy-start | bytes 9437188
  140.7 16.6 %copy-start.17 = (bf16[2,512,768]{2,1,0:T(8,128)(2,1)S(1)}, bf16[2,512,768]{2,1,0:T(8,128)(2,1)}, u32[]{:S(2)}) copy-start(bf16[2,512,768]{2,1,0:T(8,128)(2,1)} %get-tuple-element.63) | copy-start | bytes 4718596
  164.5 6.3 %copy-start.30 = (bf16[1024,3072]{1,0:T(8,128)(2,1)}, bf16[1024,3072]{1,0:T(8,128)(2,1)S(1)}, u32[]{:S(2)}) copy-start(bf16[1024,3072]{1,0:T(8,128)(2,1)S(1)} %get-tuple-element.42) | copy-start | bytes 18874372
  170.9 2.2 slice-start.2
  171.2 2.6 slice-start.3
  171.4 2.9 copy-start.4
  180.6 1.3 copy-start.21
  180.6 1.6 copy-start.22
  180.6 2.0 copy-start.23
  182.6 13.3 %copy-start.8 = (bf16[32,192,768]{2,1,0:T(8,128)(2,1)}, bf16[32,192,768]{2,1,0:T(8,128)(2,1)S(1)}, u32[]{:S(2)}) copy-start(bf16[32,192,768]{2,1,0:T(8,128)(2,1)S(1)} %constant_dynamic-update-slice_fusion) | copy-start | bytes 28311556
  195.9 3.7 copy-start.5
  199.6 1.7 copy-start.1
  199.6 2.9 copy-start.20
  199.6 5.9 %slice-start = ((s8[4718592]{0:T(1024)(128)(4,1)}), s8[4194304]{0:T(1024)(128)(4,1)S(1)}, s32[]{:S(2)}) async-start(s8[4718592]{0:T(1024)(128)(4,1)} %bitcast.228), calls=%async_computation.3 | async-start | bytes 8388608
  199.7 6.4 %slice-start.4 = ((s8[6291456]{0:T(1024)(128)(4,1)}), s8[4194304]{0:T(1024)(128)(4,1)S(1)}, s32[]{:S(2)}) async-start(s8[6291456]{0:T(1024)(128)(4,1)} %bitcast.284), calls=%async_computation.7 | async-start | bytes 8388608
  201.3 1.2 copy-start.18
  202.5 3.8 slice-start.1
  202.5 4.6 %slice-start.5 = ((s8[6291456]{0:T(1024)(128)(4,1)}), s8[2097152]{0:T(1024)(128)(4,1)S(1)}, s32[]{:S(2)}) async-start(s8[6291456]{0:T(1024)(128)(4,1)} %bitcast.284), calls=%async_computation.8 | async-start | bytes 4194304
  203.9 4.2 %copy-start.7 = (f32[1024,768]{1,0:T(8,128)S(1)}, f32[1024,768]{1,0:T(8,128)}, u32[]{:S(2)}) copy-start(f32[1024,768]{1,0:T(8,128)} %copy-done.6) | copy-start | bytes 9437188
  205.4 19.0 %collective-permute-start.3 = (bf16[1024,384]{1,0:T(8,128)(2,1)}, bf16[1024,384]{1,0:T(8,128)(2,1)}, u32[]{:S(2)}, u32[]{:S(2)}) collective-permute-start(bf16[1024,384]{1,0:T(8,128)(2,1)} %get-tuple-element.85), channel_id=1, source_target_pairs={{0,1},{1,0},{2,3},{3,2},{4,5},{5,4},{6,7},{7,6},{8,9},{9,8},{10,11... | collective-permute-start | bytes 2359304 | tf_op jit(solution)/shard_map/ppermute | solution.py:671
  217.3 154.9 %collective-permute-start.2 = (bf16[512,768]{1,0:T(8,128)(2,1)}, bf16[512,768]{1,0:T(8,128)(2,1)}, u32[]{:S(2)}, u32[]{:S(2)}) collective-permute-start(bf16[512,768]{1,0:T(8,128)(2,1)} %get-tuple-element.89), channel_id=1, source_target_pairs={{0,2},{1,3},{2,0},{3,1},{4,6},{5,7},{6,4},{7,5},{8,10},{9,11},{10,... | collective-permute-start | bytes 2359304 | tf_op jit(solution)/shard_map/ppermute | solution.py:553
  219.5 4.9 %copy-start.12 = (bf16[1024,384]{1,0:T(8,128)(2,1)S(1)}, bf16[1024,384]{1,0:T(8,128)(2,1)}, u32[]{:S(2)}) copy-start(bf16[1024,384]{1,0:T(8,128)(2,1)} %get-tuple-element.84) | copy-start | bytes 2359300
  223.1 3.7 copy-start.24
  224.1 64.1 %collective-permute-start.6 = (bf16[768,384]{1,0:T(8,128)(2,1)}, bf16[768,384]{1,0:T(8,128)(2,1)}, u32[]{:S(2)}, u32[]{:S(2)}) collective-permute-start(bf16[768,384]{1,0:T(8,128)(2,1)} %constant_dynamic-slice_fusion), channel_id=1, source_target_pairs={{0,1},{1,0},{2,3},{3,2},{4,5},{5,4},{6,7},{7,6},{8,9},{9,8},{10,11... | collective-permute-start | bytes 1769480 | tf_op jit(solution)/shard_map/ppermute | solution.py:699
  279.3 8.8 %copy-start.25 = (bf16[768,768]{1,0:T(8,128)(2,1)S(1)}, bf16[768,768]{1,0:T(8,128)(2,1)}, u32[]{:S(2)}) copy-start(bf16[768,768]{1,0:T(8,128)(2,1)} %copy-done.24) | copy-start | bytes 3538948
  286.9 5.6 %copy-start.13 = (bf16[2048,768]{1,0:T(8,128)(2,1)}, bf16[2048,768]{1,0:T(8,128)(2,1)S(1)}, u32[]{:S(2)}) copy-start(bf16[2048,768]{1,0:T(8,128)(2,1)S(1)} %convolution_convert_fusion.2) | copy-start | bytes 9437188
  286.9 4.9 %copy-start.3 = (bf16[2048,1152]{1,0:T(8,128)(2,1)S(1)}, bf16[2048,1152]{1,0:T(8,128)(2,1)}, u32[]{:S(2)}) copy-start(bf16[2048,1152]{1,0:T(8,128)(2,1)} %attend_backward.1) | copy-start | bytes 14155780
  288.1 13.6 %collective-permute-start.4 = (bf16[2,512,768]{2,1,0:T(8,128)(2,1)}, bf16[2,512,768]{2,1,0:T(8,128)(2,1)}, u32[]{:S(2)}, u32[]{:S(2)}) collective-permute-start(bf16[2,512,768]{2,1,0:T(8,128)(2,1)} %dynamic-slice_bitcast_fusion), channel_id=1, source_target_pairs={{0,1},{1,0},{2,3},{3,2},{4,5},{5,4},{6,7},{7,6},{8,9},{9,8},{10,11... | collective-permute-start | bytes 4718600 | tf_op jit(solution)/shard_map/ppermute | solution.py:679
  292.8 9.0 %copy-start.14 = (bf16[2048,768]{1,0:T(8,128)(2,1)S(1)}, bf16[2048,768]{1,0:T(8,128)(2,1)}, u32[]{:S(2)}) copy-start(bf16[2048,768]{1,0:T(8,128)(2,1)} %copy-done.13) | copy-start | bytes 9437188
  304.5 1.7 copy-start.2
  313.2 59.0 %copy-start.11 = (bf16[512,768]{1,0:T(8,128)(2,1)S(1)}, bf16[512,768]{1,0:T(8,128)(2,1)}, u32[]{:S(2)}) copy-start(bf16[512,768]{1,0:T(8,128)(2,1)} %get-tuple-element.88) | copy-start | bytes 2359300
  313.4 58.8 %collective-permute-start.5 = (bf16[512,768]{1,0:T(8,128)(2,1)S(1)}, bf16[512,768]{1,0:T(8,128)(2,1)S(1)}, u32[]{:S(2)}, u32[]{:S(2)}) collective-permute-start(bf16[512,768]{1,0:T(8,128)(2,1)S(1)} %get-tuple-element.83), channel_id=1, source_target_pairs={{0,2},{1,3},{2,0},{3,1},{4,6},{5,7},{6,4},{7,5},{8,10},{9,11},{10,... | collective-permute-start | bytes 2359304 | tf_op jit(solution)/shard_map/ppermute | solution.py:553
  372.2 3.3 copy-start.27
Sparse Core Ops, SparseCore 0:
  10.9 117.6 all-gather.1
  196.1 134.1 reduce-scatter.1

commit v2 on v1

--- a/solution.py
+++ b/solution.py
@@ -542,7 +542,7 @@
 
     def placed(both, came):
         kept = lax.dynamic_index_in_dim(both, mine, 0, keepdims=False)
-        return jnp.where((jnp.arange(micro_count) == mine)[:, None, None], kept[None], came[None])
+        return jnp.stack([jnp.where(mine == 0, kept, came), jnp.where(mine == 0, came, kept)])
 
     def own_micro(both):
         return placed(both, lax.ppermute(swap_of(both), "seq", swap_micro))
@@ -551,11 +551,11 @@
         kept = lax.dynamic_index_in_dim(blocks, mine, 0, keepdims=False)
         sent = lax.dynamic_index_in_dim(blocks, 1 - mine, 0, keepdims=False)
         came = lax.ppermute(sent, "seq", swap_micro)
-        return jnp.where((jnp.arange(micro_count) == mine)[:, None, None], kept[None], came[None])
+        return jnp.stack([jnp.where(mine == 0, kept, came), jnp.where(mine == 0, came, kept)])
 
     def interleave(own, other):
-        here = (jnp.arange(share) == core)[None, :, None, None]
-        return jnp.where(here, own[:, None], other[:, None]).reshape((bucket,) + own.shape[2:])
+        first, second = jnp.where(core == 0, own, other), jnp.where(core == 0, other, own)
+        return jnp.stack([first, second], axis=1).reshape((bucket,) + own.shape[2:])
 
 
     vectors = (gain_first, shift_first, packed_bias, output_bias, gain_second, shift_second, expand_bias, reduce_bias)

time: 393 us -> 384 us (0.977); the launches traced: 386 us -> 384 us
  Pallas kernels: 180 us -> 199 us
  starting transfers between devices: 12.2 us -> 3.49 us
  local copies, waits for them, and re-layouts: 46 us -> 38.3 us
  matrix products: 85.1 us -> 79.1 us
    pallas_call x1, Pallas kernels: 44 us -> 60.5 us  [reduce_last(): pl.pallas_call(reduce_kernel, name='reduce_last', out_shape=(jax.ShapeDty...]
    ppermute x2, starting transfers between devices: 10.5 us -> 1.18 us  [home_micro(): came = lax.ppermute(sent, 'seq', swap_micro)]
    another operation x2 -> x7, other arithmetic: 0.76 us -> 8.26 us  [the longest x4 5.5 us: home_micro(): jnp.stack([jnp.where(mine == 0, kept, came), jnp.where(mine == 0, came, k...]
    select_n x3 -> x1, other arithmetic: 8.19 us -> 1.75 us  [interleave(): jnp.where(core == 0, own, other)]
    broadcast_in_dim x7 -> x0, local copies, waits for them, and re-layouts: 5.67 us -> none  [the longest x4 2.93 us: home_micro(): jnp.where((jnp.arange(micro_count) == mine)[:, None, None], kept[None], c...]
    unnamed x96 -> x106, local copies, waits for them, and re-layouts: 11.2 us -> 9.19 us
  transfers between devices with their start and end apart: 9 -> 9, of which waited for: 1 -> 2; matrix products, arithmetic and copies ran while one was open for 25% -> 23% of each run, Pallas kernels for 46% -> 51%
where the time goes in v2:
time: 384 us
  Pallas kernels  199 us (52%)
  matrix products  79.1 us (21%)
  other arithmetic  45.4 us (12%)
  local copies, waits for them, and re-layouts  38.3 us (10%)
  between operations  15.4 us (4%)
    pallas_call x1, Pallas kernels, reduce_last(): pl.pallas_call(reduce_kernel, name='reduce_last', out_shape=(jax.ShapeDty...  60.5 us
    pallas_call x1, Pallas kernels, gather_first(): pl.pallas_call(gather_kernel, name='gather_first', out_shape=(jax.ShapeDt...  55.4 us
    pallas_call x1, Pallas kernels, attend_backward(): pl.pallas_call(attend_back_kernel, name='attend_backward', out_shape=jax....  54 us
    dot_general x4, matrix products, against_rows(): lax.dot_general(first, second, (((1,), (1,)), ((), ())), preferred_elemen...  28.1 us
    pallas_call x1, Pallas kernels, attend_forward(): pl.pallas_call(attend_kernel, name='attend_forward', out_shape=(jax.Shape...  27.2 us
    dot_general x4, matrix products, outer_sum(): lax.dot_general(first, second, (((0,), (0,)), ((), ())), preferred_elemen...  21.9 us
    dot_general x1, matrix products, local(): jnp.dot(normed_two_low, full_expand, preferred_element_type=F32)  16.6 us
    unnamed x106, local copies, waits for them, and re-layouts  9.19 us
  transfers between devices with their start and end apart: 9, of which 2 were waited for; matrix products, arithmetic and copies ran while one was open for 23% of the time, Pallas kernels for 51%

profile of v2, /device:TPU:9, one launch (start us, length us, event | category | flops | bytes accessed | tf_op | source)
XLA Modules:
  0.0 384.1 jit_solution(12884261264946733836)
XLA Ops:
  7.2 1.8 pack_second.1
  9.1 55.4 %gather_first.1 = (bf16[2,2,512,768]{3,2,1,0:T(8,128)(2,1)}, bf16[4,2,2,2,24,1152]{5,4,3,2,1,0:T(8,128)(2,1)}, f32[4,2,2,2,8,128]{5,4,3,2,1,0:T(8,128)}) custom-call(bf16[2,512,768]{2,1,0:T(8,128)(2,1)} %token_ref.1, bf16[24,2304]{1,0:T(8,128)(2,1)} %weight_ref.1, bf16[24]{0:T(256)(128)(2,1)} %rest_0_.1, bf16[24]{0:T(256)(128)(2,1)} %rest_1_.1, ...), custom_call_target="tpu_custom_call" | custom-call | tf_op jit(solution)/shard_map/gather_first/pallas_call | solution.py:370
  64.5 1.4 fusion.43
  67.3 2.1 dynamic-slice_bitcast_fusion.4
  69.4 2.4 convert_reduce_fusion.2
  72.9 1.5 add_convert_fusion.2
  74.4 5.8 %add_convert_fusion.1.packed_ref = bf16[2048,1152]{1,0:T(8,128)(2,1)} fusion(bf16[2048,768]{1,0:T(8,128)(2,1)S(1)} %bitcast.270, bf16[768,1152]{1,0:T(8,128)(2,1)S(1)} %bitcast.321, f32[1152]{0:T(1024)S(1)} %pad_maximum_fusion.11), kind=kOutput, calls=%fused_computation.7 | convolution fusion | flops 3628597248 | bytes 9638400 | tf_op jit(solution)/shard_map/dot_general | solution.py:619
  83.0 27.2 %attend_forward.1 = (bf16[2048,384]{1,0:T(8,128)(2,1)}, f32[6,2048]{1,0:T(8,128)}) custom-call(s32[2,8]{1,0:T(2,128)} %get-tuple-element.135.bounds_ref, bf16[2048,1152]{1,0:T(8,128)(2,1)} %add_convert_fusion.1.packed_ref, s32[1,2048]{1,0:T(1,128)} %bitcast.311), custom_call_target="tpu_custom_call" | custom-call | flops 3221225472 | bytes 7077888 | tf_op jit(solution)/shard_map/attend_forward/pallas_call | solution.py:129
  110.7 1.3 constant_dynamic-slice_fusion.4
  112.0 2.5 fusion.5
  117.3 1.2 fusion.23
  119.5 1.7 convert_reduce_fusion.4
  121.3 3.3 multiply_convert_fusion.2
  124.6 1.3 bitcast_select_fusion.7
  125.9 1.3 pad_maximum_fusion.1
  127.2 2.6 all-gather.2.cloned.1.call-done
  129.8 4.5 %fusion.40 = (bf16[32,24,768]{2,1,0:T(8,128)(2,1)S(1)}, bf16[32,24,768]{2,1,0:T(8,128)(2,1)}, bf16[32,24,768]{2,1,0:T(8,128)(2,1)}, bf16[32,24,768]{2,1,0:T(8,128)(2,1)}, bf16[32,24,768]{2,1,0:T(8,128)(2,1)S(1)}) fusion(bf16[32,216,768]{2,1,0:T(8,128)(2,1)} %bitcast.254), kind=kLoop, calls=%fused_computation.185 | loop fusion | bytes 11796480 | tf_op jit(solution)/shard_map/slice | solution.py:590
  134.4 3.1 slice.218
  138.1 1.6 fusion.46
  140.2 16.6 %add_convert_fusion = (bf16[1024,3072]{1,0:T(8,128)(2,1)}, bf16[1024,3072]{1,0:T(8,128)(2,1)}) fusion(f32[3072]{0:T(1024)S(1)} %add.246, bf16[768,768]{1,0:T(8,128)(2,1)} %bitcast.287, bf16[768,768]{1,0:T(8,128)(2,1)} %bitcast.289, bf16[768,768]{1,0:T(8,128)(2,1)} %bitcast.291, bf16[768,768]{1,0:T(8,128)(2,1)S(1)} %bitcast.285, ...), kind=kOutput, calls=%fused_computation.2 | convolution fusion | flops 4904976384 | bytes 20473856 | tf_op jit(solution)/shard_map/dot_general | solution.py:640
  156.8 7.2 %convert_reduce_fusion = (f32[3072]{0:T(1024)S(1)}, bf16[1024,3072]{1,0:T(8,128)(2,1)S(1)}) fusion(bf16[1024,3072]{1,0:T(8,128)(2,1)} %get-tuple-element.41, bf16[1024,768]{1,0:T(8,128)(2,1)S(1)} %bitcast.279, bf16[3072,768]{1,0:T(8,128)(2,1)S(1)} %bitcast.265), kind=kOutput, calls=%fused_computation | convolution fusion | flops 4847563776 | bytes 18886656 | tf_op jit(solution)/shard_map/dot_general | solution.py:28
  164.1 6.3 %convolution_convert_fusion.1 = bf16[768,3072]{1,0:T(8,128)(2,1)S(1)} fusion(bf16[1024,3072]{1,0:T(8,128)(2,1)S(1)} %get-tuple-element.42, f32[1024,768]{1,0:T(8,128)S(1)} %get-tuple-element.131, f32[768]{0:T(1024)S(1)} %add.243, f32[768]{0:T(1024)S(1)} %mul.289, f32[1024]{0:T(1024)S(1)} %fusion.28, f32[1024]{0:T(1024)S(1)} %broadcast_multiply_fusion.2), kind=kOutput, calls=%fused_computation.17 | convolution fusion | flops 4838129664 | bytes 14170112 | tf_op jit(solution)/shard_map/dot_general | solution.py:24
  171.3 1.3 slice-done.2
  173.8 5.9 %convolution_convert_fusion = bf16[3072,768]{1,0:T(8,128)(2,1)S(1)} fusion(bf16[1024,3072]{1,0:T(8,128)(2,1)S(1)} %bitcast.323, bf16[1024,768]{1,0:T(8,128)(2,1)S(1)} %copy-done.20), kind=kOutput, calls=%fused_computation.16 | convolution fusion | flops 4834197504 | bytes 12582912 | tf_op jit(solution)/shard_map/dot_general | solution.py:24
  181.4 12.0 %multiply_reduce_fusion.1 = (f32[768]{0:T(1024)S(1)}, f32[1024]{0:T(1024)S(1)}, f32[768]{0:T(1024)S(1)}, f32[1024,768]{1,0:T(8,128)S(1)}) fusion(f32[1024,768]{1,0:T(8,128)S(1)} %get-tuple-element.131, f32[1024]{0:T(1024)S(1)} %fusion.28, f32[1024]{0:T(1024)S(1)} %broadcast_multiply_fusion.2, f32[768]{0:T(1024)S(1)} %mul.289, ...), kind=kOutput, calls=%fused_computation.47 | convolution fusion | flops 4857000960 | bytes 17323008 | tf_op jit(solution)/shard_map/dot_general | solution.py:28
  193.4 2.6 fusion.39
  196.0 3.2 convert_reduce_fusion.5
  199.3 1.4 convolution_convert_fusion.4
  202.0 1.5 convolution_convert_fusion.5
  205.0 5.1 %multiply_convert_fusion.4 = bf16[1024,768]{1,0:T(8,128)(2,1)S(1)} fusion(f32[1024,768]{1,0:T(8,128)S(1)} %copy-done.8, bf16[1024,3072]{1,0:T(8,128)(2,1)S(1)} %bitcast.325, bf16[3072,768]{1,0:T(8,128)(2,1)S(1)} %bitcast.268, f32[1024]{0:T(1024)S(1)} %bitcast.300, f32[768]{0:T(1024)S(1)} %add.255), kind=kOutput, calls=%fused_computation.54 | convolution fusion | flops 4835770368 | bytes 15735808 | tf_op jit(solution)/shard_map/dot_general | solution.py:643
  213.7 2.2 add_convert_fusion.4
  215.9 1.7 broadcast_select_fusion.1
  217.7 1.3 pad_maximum_fusion.4
  219.0 54.0 %attend_backward.1 = bf16[2048,1152]{1,0:T(8,128)(2,1)} custom-call(s32[2,8]{1,0:T(2,128)} %get-tuple-element.136.bounds_ref, bf16[2048,1152]{1,0:T(8,128)(2,1)} %add_convert_fusion.1.packed_ref, bf16[2048,384]{1,0:T(8,128)(2,1)} %get-tuple-element.38.o_ref, bf16[2048,384]{1,0:T(8,128)(2,1)} %bitcast.256, s32[1,2048]{1,0:T(1,128)} %bitcast.312, ...), custom_call_target="tpu_custom_call" | custom-call | flops 12582912 | bytes 2359296 | tf_op jit(solution)/shard_map/attend_backward/pallas_call | solution.py:234
  273.0 7.5 %convolution_convert_fusion.2 = bf16[2048,768]{1,0:T(8,128)(2,1)S(1)} fusion(bf16[2048,1152]{1,0:T(8,128)(2,1)} %attend_backward.1, bf16[768,1152]{1,0:T(8,128)(2,1)} %bitcast.320), kind=kOutput, calls=%fused_computation.22 | convolution fusion | flops 3625451520 | bytes 9633792 | tf_op jit(solution)/shard_map/dot_general | solution.py:28
  280.5 1.4 dynamic-slice_bitcast_fusion
  283.5 1.6 fusion.25
  285.2 1.3 pad_maximum_fusion.2
  286.5 8.2 %convolution_convert_fusion.3 = bf16[768,1152]{1,0:T(8,128)(2,1)} fusion(bf16[2048,768]{1,0:T(8,128)(2,1)S(1)} %copy-done.15, bf16[2048,1152]{1,0:T(8,128)(2,1)} %attend_backward.1), kind=kOutput, calls=%fused_computation.23 | convolution fusion | flops 3624763392 | bytes 9633792 | tf_op jit(solution)/shard_map/dot_general | solution.py:24
  294.7 2.7 fusion.17
  297.5 1.6 fusion.16
  299.7 2.3 fusion.8
  304.4 60.5 %reduce_last.1 = (f32[24,1152]{1,0:T(8,128)}, f32[24,1152]{1,0:T(8,128)}, f32[24,384]{1,0:T(8,128)}, f32[24,384]{1,0:T(8,128)}, f32[8,128]{1,0:T(8,128)}) custom-call(bf16[4,2,2,48,1152]{4,3,2,1,0:T(8,128)(2,1)} %bitcast.276, bf16[4,2,2,48,384]{4,3,2,1,0:T(8,128)(2,1)} %bitcast.275, f32[4,2,2,16,128]{4,3,2,1,0:T(8,128)} %bitcast.293), custom_call_target="tpu_custom_call" | custom-call | tf_op jit(solution)/shard_map/reduce_last/pallas_call | solution.py:463
  364.8 1.2 slice_bitcast_fusion.5
  367.2 1.4 slice_bitcast_fusion
  371.2 1.3 fusion.21
  372.5 1.3 pad_maximum_fusion.5
  375.4 1.6 slice.236
  (201 shorter events, 30.3 us)
Async XLA Ops:
  7.2 122.7 %all-gather.2.cloned.1.call-start = ((), (), s32[]{:S(2)}) async-start(), calls=%async_computation.1 | async-start | bytes 10948608 | tf_op jit(solution)/shard_map/all_gather | solution.py:504
  9.0 364.8 %reduce-scatter.2.cloned.1.call-start = ((), (), s32[]{:S(2)}) async-start(), calls=%async_computation.2 | async-start | bytes 9732096 | tf_op jit(solution)/shard_map/reduce_scatter | solution.py:508
  64.5 7.3 %copy-start = (bf16[2,2,512,768]{3,2,1,0:T(8,128)(2,1)S(1)}, bf16[2,2,512,768]{3,2,1,0:T(8,128)(2,1)}, u32[]{:S(2)}) copy-start(bf16[2,2,512,768]{3,2,1,0:T(8,128)(2,1)} %get-tuple-element.32) | copy-start | bytes 9437188
  72.9 1.5 copy-start.34
  74.4 5.8 %copy-start.33 = (s32[2,1,4]{2,1,0:T(1,128)S(1)}, s32[2,1,4]{2,1,0:T(1,128)}, u32[]{:S(2)}) copy-start(s32[2,1,4]{2,1,0:T(1,128)} %param.17) | copy-start | bytes 100
  80.2 35.0 %collective-permute-start = (bf16[512,768]{1,0:T(8,128)(2,1)}, bf16[512,768]{1,0:T(8,128)(2,1)}, u32[]{:S(2)}, u32[]{:S(2)}) collective-permute-start(bf16[512,768]{1,0:T(8,128)(2,1)} %dynamic-slice_bitcast_fusion.4), channel_id=1, source_target_pairs={{0,2},{1,3},{2,0},{3,1},{4,6},{5,7},{6,4},{7,5},{8,10},{9,11},{10,... | collective-permute-start | bytes 2359304 | tf_op jit(solution)/shard_map/ppermute | solution.py:623
  80.5 2.4 copy-start.31
  112.0 3.2 copy-start.10
  112.0 5.3 %copy-start.22 = (bf16[2,512,768]{2,1,0:T(8,128)(2,1)S(1)}, bf16[2,512,768]{2,1,0:T(8,128)(2,1)}, u32[]{:S(2)}) copy-start(bf16[2,512,768]{2,1,0:T(8,128)(2,1)} %param.16) | copy-start | bytes 4718596
  116.2 8.4 %collective-permute-start.1 = (bf16[2,512,384]{2,1,0:T(8,128)(2,1)}, bf16[2,512,384]{2,1,0:T(8,128)(2,1)}, u32[]{:S(2)}, u32[]{:S(2)}) collective-permute-start(bf16[2,512,384]{2,1,0:T(8,128)(2,1)} %dynamic-slice_bitcast_fusion.3), channel_id=1, source_target_pairs={{0,1},{1,0},{2,3},{3,2},{4,5},{5,4},{6,7},{7,6},{8,9},{9,8},{10,11... | collective-permute-start | bytes 2359304 | tf_op jit(solution)/shard_map/ppermute | solution.py:629
  118.6 2.6 copy-start.4
  121.3 3.3 copy-start.11
  134.4 3.1 copy-start.26
  134.4 3.3 copy-start.18
  134.4 3.7 copy-start.25
  137.5 19.3 %copy-start.14 = (bf16[32,96,768]{2,1,0:T(8,128)(2,1)}, bf16[32,96,768]{2,1,0:T(8,128)(2,1)S(1)}, u32[]{:S(2)}) copy-start(bf16[32,96,768]{2,1,0:T(8,128)(2,1)S(1)} %slice.218) | copy-start | bytes 14155780
  139.7 53.7 %copy-start.7 = (f32[1024,768]{1,0:T(8,128)}, f32[1024,768]{1,0:T(8,128)S(1)}, u32[]{:S(2)}) copy-start(f32[1024,768]{1,0:T(8,128)S(1)} %get-tuple-element.131) | copy-start | bytes 9437188
  140.2 16.6 %copy-start.21 = (bf16[2,512,768]{2,1,0:T(8,128)(2,1)S(1)}, bf16[2,512,768]{2,1,0:T(8,128)(2,1)}, u32[]{:S(2)}) copy-start(bf16[2,512,768]{2,1,0:T(8,128)(2,1)} %get-tuple-element.63) | copy-start | bytes 4718596
  164.0 6.3 %copy-start.35 = (bf16[1024,3072]{1,0:T(8,128)(2,1)}, bf16[1024,3072]{1,0:T(8,128)(2,1)S(1)}, u32[]{:S(2)}) copy-start(bf16[1024,3072]{1,0:T(8,128)(2,1)S(1)} %get-tuple-element.42) | copy-start | bytes 18874372
  170.4 2.2 slice-start.2
  170.7 2.6 slice-start.3
  170.9 2.9 copy-start.20
  179.7 1.3 copy-start.28
  179.7 1.6 copy-start.29
  181.4 12.0 %copy-start.9 = (bf16[32,192,768]{2,1,0:T(8,128)(2,1)}, bf16[32,192,768]{2,1,0:T(8,128)(2,1)S(1)}, u32[]{:S(2)}) copy-start(bf16[32,192,768]{2,1,0:T(8,128)(2,1)S(1)} %constant_dynamic-update-slice_fusion) | copy-start | bytes 28311556
  196.0 3.2 copy-start.27
  196.0 8.9 %slice-start = ((s8[4718592]{0:T(1024)(128)(4,1)}), s8[4194304]{0:T(1024)(128)(4,1)S(1)}, s32[]{:S(2)}) async-start(s8[4718592]{0:T(1024)(128)(4,1)} %bitcast.266), calls=%async_computation.3 | async-start | bytes 8388608
  196.0 8.9 %slice-start.4 = ((s8[6291456]{0:T(1024)(128)(4,1)}), s8[4194304]{0:T(1024)(128)(4,1)S(1)}, s32[]{:S(2)}) async-start(s8[6291456]{0:T(1024)(128)(4,1)} %bitcast.324), calls=%async_computation.7 | async-start | bytes 8388608
  199.2 2.7 copy-start.19
  199.3 5.7 %slice-start.1 = ((s8[4718592]{0:T(1024)(128)(4,1)}), s8[524288]{0:T(1024)(128)(4,1)S(1)}, s32[]{:S(2)}) async-start(s8[4718592]{0:T(1024)(128)(4,1)} %bitcast.266), calls=%async_computation.4 | async-start | bytes 1048576
  199.3 5.7 %slice-start.5 = ((s8[6291456]{0:T(1024)(128)(4,1)}), s8[2097152]{0:T(1024)(128)(4,1)S(1)}, s32[]{:S(2)}) async-start(s8[6291456]{0:T(1024)(128)(4,1)} %bitcast.324), calls=%async_computation.8 | async-start | bytes 4194304
  200.7 2.7 copy-start.24
  201.7 3.2 copy-start.8
  201.7 14.2 %collective-permute-start.3 = (bf16[1024,384]{1,0:T(8,128)(2,1)}, bf16[1024,384]{1,0:T(8,128)(2,1)}, u32[]{:S(2)}, u32[]{:S(2)}) collective-permute-start(bf16[1024,384]{1,0:T(8,128)(2,1)} %constant_dynamic-slice_fusion.1), channel_id=1, source_target_pairs={{0,1},{1,0},{2,3},{3,2},{4,5},{5,4},{6,7},{7,6},{8,9},{9,8},{10,11... | collective-permute-start | bytes 2359304 | tf_op jit(solution)/shard_map/ppermute | solution.py:671
  203.4 1.2 copy-start.30
  204.7 9.0 %collective-permute-start.6 = (bf16[768,384]{1,0:T(8,128)(2,1)}, bf16[768,384]{1,0:T(8,128)(2,1)}, u32[]{:S(2)}, u32[]{:S(2)}) collective-permute-start(bf16[768,384]{1,0:T(8,128)(2,1)} %constant_dynamic-slice_fusion), channel_id=1, source_target_pairs={{0,1},{1,0},{2,3},{3,2},{4,5},{5,4},{6,7},{7,6},{8,9},{9,8},{10,11... | collective-permute-start | bytes 1769480 | tf_op jit(solution)/shard_map/ppermute | solution.py:699
  212.2 71.3 %collective-permute-start.2 = (bf16[512,768]{1,0:T(8,128)(2,1)}, bf16[512,768]{1,0:T(8,128)(2,1)}, u32[]{:S(2)}, u32[]{:S(2)}) collective-permute-start(bf16[512,768]{1,0:T(8,128)(2,1)} %dynamic-slice_bitcast_fusion.2), channel_id=1, source_target_pairs={{0,2},{1,3},{2,0},{3,1},{4,6},{5,7},{6,4},{7,5},{8,10},{9,11},{10,... | collective-permute-start | bytes 2359304 | tf_op jit(solution)/shard_map/ppermute | solution.py:553
  273.0 9.5 %copy-start.6 = (bf16[2048,1152]{1,0:T(8,128)(2,1)S(1)}, bf16[2048,1152]{1,0:T(8,128)(2,1)}, u32[]{:S(2)}) copy-start(bf16[2048,1152]{1,0:T(8,128)(2,1)} %attend_backward.1) | copy-start | bytes 14155780
  280.5 2.7 copy-start.16
  281.9 12.8 %collective-permute-start.4 = (bf16[2,512,768]{2,1,0:T(8,128)(2,1)}, bf16[2,512,768]{2,1,0:T(8,128)(2,1)}, u32[]{:S(2)}, u32[]{:S(2)}) collective-permute-start(bf16[2,512,768]{2,1,0:T(8,128)(2,1)} %dynamic-slice_bitcast_fusion), channel_id=1, source_target_pairs={{0,1},{1,0},{2,3},{3,2},{4,5},{5,4},{6,7},{7,6},{8,9},{9,8},{10,11... | collective-permute-start | bytes 4718600 | tf_op jit(solution)/shard_map/ppermute | solution.py:679
  283.5 2.9 copy-start.15
  286.5 8.2 %copy-start.17 = (bf16[2048,768]{1,0:T(8,128)(2,1)S(1)}, bf16[2048,768]{1,0:T(8,128)(2,1)}, u32[]{:S(2)}) copy-start(bf16[2048,768]{1,0:T(8,128)(2,1)} %copy-done.16) | copy-start | bytes 9437188
  297.4 1.9 copy-start.1
  297.4 2.1 copy-start.3
  297.4 2.3 copy-start.5
  303.2 67.9 %copy-start.13 = (bf16[1024,768]{1,0:T(8,128)(2,1)S(1)}, bf16[1024,768]{1,0:T(8,128)(2,1)}, u32[]{:S(2)}) copy-start(bf16[1024,768]{1,0:T(8,128)(2,1)} %copy-done.12) | copy-start | bytes 4718596
  303.3 67.9 %collective-permute-start.5 = (bf16[512,768]{1,0:T(8,128)(2,1)S(1)}, bf16[512,768]{1,0:T(8,128)(2,1)}, u32[]{:S(2)}, u32[]{:S(2)}) collective-permute-start(bf16[512,768]{1,0:T(8,128)(2,1)S(1)} %dynamic-slice_bitcast_fusion.1), channel_id=1, source_target_pairs={{0,2},{1,3},{2,0},{3,1},{4,6},{5,7},{6,4},{7,5},{8,10},{9,11},{10,... | collective-permute-start | bytes 2359304 | tf_op jit(solution)/shard_map/ppermute | solution.py:553
  371.1 2.6 copy-start.32
  (3 other events, 3.2 us)
Sparse Core Ops, SparseCore 0:
  10.9 118.8 all-gather.1
  196.1 135.3 reduce-scatter.1
